TPU v7x, 32 devices: a whole 2x2x4 slice. The times are simulated.
32 devices in a mesh: sx: 8 (over z, core), sy: 4 (over y, x).
Axes of the slice: x: 2, y: 2, z: 4, core: 2. Of those that a mesh axis runs over, the one named last changes fastest.
Arguments:
- weights: float32 [8, 16, 32, 16, 128], P(None, None, 'sx', 'sy'), may hold values from -0.6 to 0.6
Outputs:
- outgoing: float32 [2, 64, 2, 128, 2, 1, 128], P(None, 'sx', None, 'sy')
All inputs are finite; a program needn't handle non-finite values.
Results may differ from a plain program's by a relative error of at most 0.0075.
Values sent between devices are 32-bit elements; how exact they have to be, the bound alone decides.
No kernel may reach another device: no remote copies, remote signals or barrier semaphores. Data moves between devices by JAX's collectives and lax.ppermute only.
A program may use at most 64 MiB of HBM per device.

v0:
```python
import math

import jax
import jax.numpy as jnp
from jax import lax
from jax.sharding import PartitionSpec as P

GRID = 4096
BOXES = 64


two_pi = 2.0 * math.pi


def swapped(block, axis, distance):
    count = lax.axis_size(axis)
    route = []
    for low in range(count):
        high = low | 1 << distance
        if high != low and high < count:
            route += [(low, high), (high, low)]
    return lax.ppermute(block, axis, route)


def chebyshev_nodes():
    counter = jnp.arange(8, dtype=jnp.float32)
    return 0.5 - 0.5 * jnp.cos(math.pi * (2.0 * counter + 1.0) / 16.0)


def lagrange_child(points, child_side):
    shifted = (child_side + points) / 2.0
    numerator = shifted[None, :, None] - points[None, None, :]
    denominator = points[:, None] - points[None, :]
    diagonal_mask = jnp.eye(8, dtype=bool)
    numerator = jnp.where(diagonal_mask[:, None, :], 1.0, numerator)
    denominator = jnp.where(diagonal_mask, 1.0, denominator)
    return jnp.prod(numerator / denominator[:, None, :], axis=2)


def child_blocks():
    points = chebyshev_nodes()
    stacked = []
    for side_x in range(2):
        for side_y in range(2):
            kernel = jnp.kron(lagrange_child(points, side_x), lagrange_child(points, side_y))
            transposed = kernel.T
            zero_block = jnp.zeros((64, 64), jnp.float32)
            stacked.append(jnp.block([[transposed, zero_block], [zero_block, transposed]]))
    return jnp.concatenate(stacked, axis=0)


def centers(first_box, how_many, boxes_all):
    return (
        (first_box + jnp.arange(how_many, dtype=jnp.int32)).astype(jnp.float32) + 0.5
    ) / boxes_all


def split_centers(position, piece, span, boxes_all):
    counter = jnp.arange(4 * piece, dtype=jnp.int32)
    global_row = (
        counter // (2 * piece) * (2 * span) + position * (2 * piece) + counter % (2 * piece)
    )
    return (global_row.astype(jnp.float32) + 0.5) / boxes_all


def box_points(first_box, how_many, boxes_all, points):
    anchor = (first_box + jnp.arange(how_many, dtype=jnp.int32)).astype(jnp.float32)
    return (anchor[:, None] + points[None, :]) / boxes_all


def phase_of(x_centers, y_centers, points_x, points_y):
    coord_x = x_centers[:, None, None, None, None, None]
    coord_y = y_centers[None, :, None, None, None, None]
    freq_x = points_x[None, None, :, None, :, None]
    freq_y = points_y[None, None, None, :, None, :]
    speed_map = (2.0 + jnp.sin(two_pi * coord_x) * jnp.sin(two_pi * coord_y)) / 3.0
    cycles = GRID * (
        coord_x * freq_x
        + coord_y * freq_y
        + speed_map * jnp.sqrt(freq_x * freq_x + freq_y * freq_y)
    )
    angles = two_pi * (cycles - jnp.floor(cycles))
    return angles.reshape(
        x_centers.shape[0], y_centers.shape[0], points_x.shape[0], points_y.shape[0], 64
    )


def rotate(values, angles):
    cosine = jnp.cos(angles)
    sine_part = jnp.sin(angles)
    real_part = values[..., :64]
    imag_part = values[..., 64:]
    return jnp.concatenate(
        [cosine * real_part - sine_part * imag_part, sine_part * real_part + cosine * imag_part],
        axis=-1,
    )


def advance(widened, x_centers, y_centers, child_px, child_py, parent_px, parent_py, child_mix):
    turned = rotate(widened, -phase_of(x_centers, y_centers, child_px, child_py))
    dims_now = turned.shape
    boxes_x = dims_now[2] // 2
    boxes_y = dims_now[3] // 2
    grouped = turned.reshape(dims_now[0], dims_now[1], boxes_x, 2, boxes_y, 2, 128)
    grouped = grouped.transpose(0, 1, 2, 4, 3, 5, 6).reshape(
        dims_now[0], dims_now[1], boxes_x, boxes_y, 512
    )
    combined = jnp.dot(
        grouped, child_mix, precision=lax.Precision.HIGHEST, preferred_element_type=jnp.float32
    )
    return rotate(combined, phase_of(x_centers, y_centers, parent_px, parent_py))


def double_up(values):
    return jnp.repeat(jnp.repeat(values, 2, axis=0), 2, axis=1)


def move_to_targets(pieces, count_x, count_y):
    dims_now = pieces.shape
    flattened = pieces.transpose(0, 2, 1, 3, 4).reshape(
        count_x * count_y, dims_now[1], dims_now[3], 128
    )
    shuffled = lax.all_to_all(flattened, ("sx", "sy"), split_axis=0, concat_axis=0, tiled=True)
    arrived = shuffled.reshape(count_x, count_y, dims_now[1], dims_now[3], 128).transpose(
        0, 2, 1, 3, 4
    )
    return arrived


def on_device(weights):
    count_x = lax.axis_size("sx")
    count_y = lax.axis_size("sy")
    pos_x = lax.axis_index("sx")
    pos_y = lax.axis_index("sy")
    child_mix = child_blocks()
    points = chebyshev_nodes()
    base_x = weights.shape[0]
    base_y = weights.shape[1]
    top_boxes = GRID // BOXES
    first_level = advance(
        double_up(weights),
        centers(0, 2 * base_x, 2 * top_boxes),
        centers(0, 2 * base_y, 2 * top_boxes),
        box_points(4 * pos_x, 4, BOXES, points),
        box_points(4 * pos_y, 4, BOXES, points),
        box_points(2 * pos_x, 2, BOXES // 2, points),
        box_points(2 * pos_y, 2, BOXES // 2, points),
        child_mix,
    )
    second_level = advance(
        double_up(first_level),
        centers(0, 4 * base_x, 4 * top_boxes),
        centers(0, 4 * base_y, 4 * top_boxes),
        box_points(2 * pos_x, 2, BOXES // 2, points),
        box_points(2 * pos_y, 2, BOXES // 2, points),
        box_points(pos_x, 1, BOXES // 4, points),
        box_points(pos_y, 1, BOXES // 4, points),
        child_mix,
    )
    span_x = 4 * base_x
    span_y = 4 * base_y
    piece_x = span_x // count_x
    piece_y = span_y // count_y
    bit_x = pos_x % 2
    bit_y = pos_y % 2
    par_x = pos_x // 2
    par_y = pos_y // 2
    kept_x = centers(bit_x * span_x, span_x, 8 * top_boxes)
    kept_y = centers(bit_y * span_y, span_y, 8 * top_boxes)
    parent_px = box_points(par_x, 1, BOXES // 8, points)
    parent_py = box_points(par_y, 1, BOXES // 8, points)
    widened = double_up(second_level)
    turned = rotate(
        widened,
        -phase_of(
            centers(0, 2 * span_x, 8 * top_boxes),
            centers(0, 2 * span_y, 8 * top_boxes),
            box_points(pos_x, 1, BOXES // 4, points),
            box_points(pos_y, 1, BOXES // 4, points),
        ),
    )
    child_index = 2 * bit_x + bit_y
    child_rows = lax.dynamic_slice_in_dim(child_mix, child_index * 128, 128, 0)
    partials = jnp.dot(
        turned, child_rows, precision=lax.Precision.HIGHEST, preferred_element_type=jnp.float32
    )
    keep_x = lax.dynamic_slice_in_dim(partials, bit_x * span_x, span_x, 0)
    give_x = lax.dynamic_slice_in_dim(partials, (1 - bit_x) * span_x, span_x, 0)
    summed_x = keep_x + swapped(give_x, "sx", 0)
    keep_y = lax.dynamic_slice_in_dim(summed_x, bit_y * span_y, span_y, 1)
    give_y = lax.dynamic_slice_in_dim(summed_x, (1 - bit_y) * span_y, span_y, 1)
    summed = keep_y + swapped(give_y, "sy", 0)
    third_level = rotate(summed, phase_of(kept_x, kept_y, parent_px, parent_py))
    pieces = third_level.reshape(count_x, piece_x, count_y, piece_y, 128)
    arrived = move_to_targets(pieces, count_x, count_y)
    regrouped = arrived.reshape(count_x // 2, 2, piece_x, count_y // 2, 2, piece_y, 128)
    regrouped = regrouped.transpose(1, 2, 4, 5, 0, 3, 6).reshape(
        2 * piece_x, 2 * piece_y, count_x // 2, count_y // 2, 128
    )
    last_level = advance(
        double_up(regrouped),
        split_centers(pos_x, piece_x, span_x, 16 * top_boxes),
        split_centers(pos_y, piece_y, span_y, 16 * top_boxes),
        box_points(0, count_x // 2, BOXES // 8, points),
        box_points(0, count_y // 2, BOXES // 8, points),
        box_points(0, count_x // 4, BOXES // 16, points),
        box_points(0, count_y // 4, BOXES // 16, points),
        child_mix,
    )
    return last_level.reshape(2, 2 * piece_x, 2, 2 * piece_y, count_x // 4, count_y // 4, 128)


def solution(mesh):
    placed = (P(None, None, "sx", "sy", None),)
    return jax.shard_map(
        on_device,
        mesh=mesh,
        in_specs=placed,
        out_specs=P(None, "sx", None, "sy", None, None, None),
        check_vma=False,
    )
```

profile of v0, /device:TPU:0, one launch (start us, length us, event | category | flops | bytes accessed | tf_op | source)
XLA Modules:
  0.0 240.8 jit_solution(16949873981828549205)
XLA Ops:
  6.3 17.3 %multiply_subtract_fusion.3 = (f32[16,32,4,4,64]{4,1,3,2,0:T(8,128)S(1)}, f32[16,32,4,4,64]{4,1,3,2,0:T(8,128)S(1)}) fusion(f32[16,32,4,4,128]{4,1,3,2,0:T(8,128)S(1)} %bitcast.114, f32[4,4,64]{2,1,0:T(4,128)S(1)} %add_sqrt_fusion, f32[16,32]{1,0:T(8,128)S(1)} %add_multiply_fusion.3, f32[32,4,64]{2,0,1:T(8,128)S(1)} %copy.99, f32[16,4,64]{2,1,0:T(4,128)S(1)} %copy.98), kind=kLoop, calls=%fused_computation.28 | loop fusion | flops 7340032 | bytes 8443904 | tf_op jit(solution)/shard_map/sub | solution.py:94
  24.7 5.8 %copy.101 = f32[16,32,2,2,2,2,128]{6,5,4,1,3,2,0:T(2,128)} copy(f32[16,32,2,2,2,2,128]{6,1,5,3,4,2,0:T(8,128)S(1)} %bitcast.117) | data formatting | bytes 8388608 | tf_op jit(solution)/shard_map/transpose | solution.py:105
  30.5 6.4 %reshape.1681 = f32[16,32,2,2,512]{4,1,3,2,0:T(8,128)} reshape(f32[16,32,2,2,2,2,128]{6,5,4,1,3,2,0:T(2,128)} %copy.101) | data formatting | bytes 8388608 | tf_op jit(solution)/shard_map/reshape | solution.py:105
  38.4 5.9 %fusion.37 = f32[16,32,2,2,128]{4,1,3,2,0:T(8,128)S(1)} fusion(f32[16,32,2,2,512]{4,1,3,2,0:T(8,128)} %reshape.1681, f32[512,128]{1,0:T(8,128)S(1)} %pad_dynamic-update-slice_fusion), kind=kOutput, calls=%fused_computation.71 | convolution fusion | flops 1610612736 | bytes 5505024 | tf_op jit(solution)/shard_map/dot_general | solution.py:108
  44.3 4.5 %multiply_subtract_fusion.7 = (f32[16,32,2,2,64]{4,1,3,2,0:T(8,128)S(1)}, f32[16,32,2,2,64]{4,1,3,2,0:T(8,128)S(1)}) fusion(f32[16,32,2,2,128]{4,1,3,2,0:T(8,128)S(1)} %fusion.37, f32[2,2,64]{2,1,0:T(2,128)S(1)} %add_sqrt_fusion.2, f32[16,32]{1,0:T(8,128)S(1)} %add_multiply_fusion.3, f32[32,2,64]{2,0,1:T(8,128)S(1)} %copy.97, f32[16,2,64]{2,1,0:T(2,128)S(1)} %copy.96), kind=kLoop, calls=%fused_computation.61 | loop fusion | flops 1703936 | bytes 2124800 | tf_op jit(solution)/shard_map/sub | solution.py:94
  51.4 17.6 %multiply_subtract_fusion.2 = (f32[32,64,2,2,64]{4,1,3,2,0:T(8,128)S(1)}, f32[32,64,2,2,64]{4,1,3,2,0:T(8,128)S(1)}) fusion(f32[32,64,2,2,128]{4,1,3,2,0:T(8,128)S(1)} %bitcast.115, f32[2,2,64]{2,1,0:T(2,128)S(1)} %add_sqrt_fusion.2, f32[32,64]{1,0:T(8,128)S(1)} %add_multiply_fusion.1, f32[64,2,64]{2,0,1:T(8,128)S(1)} %copy.95, f32[32,2,64]{2,1,0:T(2,128)S(1)} %copy.94), kind=kLoop, calls=%fused_computation.26 | loop fusion | flops 7340032 | bytes 8446976 | tf_op jit(solution)/shard_map/sub | solution.py:94
  70.1 5.2 %copy.106 = f32[32,64,2,2,128]{4,3,2,1,0:T(2,128)} copy(f32[32,64,2,2,128]{4,1,3,2,0:T(8,128)S(1)} %pad_maximum_fusion.1) | data formatting | bytes 8388608 | tf_op jit(solution)/shard_map/concatenate | solution.py:93
  75.3 6.5 %reshape.1684 = f32[32,64,512]{2,1,0:T(8,128)} reshape(f32[32,64,2,2,128]{4,3,2,1,0:T(2,128)} %copy.106) | data formatting | bytes 8388608 | tf_op jit(solution)/shard_map/reshape.107
  81.8 5.5 %convolution_bitcast_fusion = f32[32,64,1,1,128]{4,1,0,3,2:T(8,128)S(1)} fusion(f32[32,64,512]{2,1,0:T(8,128)} %reshape.1684, f32[512,128]{1,0:T(8,128)S(1)} %pad_dynamic-update-slice_fusion), kind=kOutput, calls=%fused_computation.44 | convolution fusion | flops 1610612736 | bytes 5505024 | tf_op jit(solution)/shard_map/dot_general | solution.py:108
  88.3 4.5 %multiply_subtract_fusion.6 = (f32[32,64,1,1,64]{4,1,0,3,2:T(8,128)S(1)}, f32[32,64,1,1,64]{4,1,0,3,2:T(8,128)S(1)}) fusion(f32[32,64,1,1,128]{4,1,0,3,2:T(8,128)S(1)} %convolution_bitcast_fusion, f32[64]{0:T(128)S(1)} %add_sqrt_fusion.4, f32[32,64]{1,0:T(8,128)S(1)} %add_multiply_fusion.1, f32[64,64]{1,0:T(8,128)S(1)} %copy.93, f32[32,64]{1,0:T(8,128)S(1)} %copy.92), kind=kLoop, calls=%fused_computation.59 | loop fusion | flops 1703936 | bytes 2130176 | tf_op jit(solution)/shard_map/sub | solution.py:94
  95.1 16.8 %multiply_subtract_fusion.1 = (f32[64,128,1,1,64]{4,1,0,3,2:T(8,128)S(1)}, f32[64,128,1,1,64]{4,1,0,3,2:T(8,128)S(1)}) fusion(f32[64,128,1,1,128]{4,1,0,3,2:T(8,128)S(1)} %bitcast.113, f32[64]{0:T(128)S(1)} %add_sqrt_fusion.4, f32[64,128]{1,0:T(8,128)S(1)} %add_multiply_fusion, f32[128,64]{1,0:T(8,128)S(1)} %copy.91, f32[64,64]{1,0:T(8,128)S(1)} %copy.90), kind=kLoop, calls=%fused_computation.24 | loop fusion | flops 7340032 | bytes 8470784 | tf_op jit(solution)/shard_map/sub | solution.py:94
  111.9 3.8 %fusion.8 = f32[64,128,128]{2,1,0:T(8,128)S(1)} fusion(f32[64,128,1,1,64]{4,1,0,3,2:T(8,128)S(1)} %get-tuple-element.8, f32[64,128,1,1,64]{4,1,0,3,2:T(8,128)S(1)} %get-tuple-element.7, f32[512,128]{1,0:T(8,128)S(1)} %pad_dynamic-update-slice_fusion, s32[]{:T(128)S(6)} %select_n.124), kind=kOutput, calls=%fused_computation.15 | convolution fusion | flops 1611661312 | bytes 12648452 | tf_op jit(solution)/shard_map/dot_general | solution.py:184
  119.3 3.0 %collective-permute-done = f32[32,128,1,1,128]{4,1,0,3,2:T(8,128)} collective-permute-done((f32[32,128,1,1,128]{4,1,0,3,2:T(8,128)S(1)}, f32[32,128,1,1,128]{4,1,0,3,2:T(8,128)}, u32[]{:S(2)}, u32[]{:S(2)}) %collective-permute-start) | collective-permute-done | bytes 2097184 | tf_op jit(solution)/shard_map/ppermute | solution.py:22
  122.3 2.5 %bitcast_add_fusion = f32[32,128,1,1,128]{4,1,0,3,2:T(8,128)S(1)} fusion(f32[32,128,1,1,128]{4,1,0,3,2:T(8,128)} %collective-permute-done, f32[64,128,128]{2,1,0:T(8,128)} %copy-done, s32[]{:T(128)S(6)} %select_n.125), kind=kLoop, calls=%fused_computation.37 | loop fusion | flops 524288 | bytes 6291460 | tf_op jit(solution)/shard_map/add | solution.py:189
  124.9 2.9 %collective-permute-start.1 = (f32[32,64,1,1,128]{4,1,0,3,2:T(8,128)S(1)}, f32[32,64,1,1,128]{4,1,0,3,2:T(8,128)}, u32[]{:S(2)}, u32[]{:S(2)}) collective-permute-start(f32[32,64,1,1,128]{4,1,0,3,2:T(8,128)S(1)} %constant_dynamic-slice_fusion), channel_id=1, source_target_pairs={{0,1},{1,0},{2,3},{3,2},{4,5},{5,4},{6,7},{7,6},{8,9},{9,8},{10,11... | collective-permute-start | bytes 3145736 | tf_op jit(solution)/shard_map/ppermute | solution.py:22
  129.6 21.7 %collective-permute-done.1 = f32[32,64,1,1,128]{4,1,0,3,2:T(8,128)} collective-permute-done((f32[32,64,1,1,128]{4,1,0,3,2:T(8,128)S(1)}, f32[32,64,1,1,128]{4,1,0,3,2:T(8,128)}, u32[]{:S(2)}, u32[]{:S(2)}) %collective-permute-start.1) | collective-permute-done | bytes 1048608 | tf_op jit(solution)/shard_map/ppermute | solution.py:22
  152.7 5.3 %multiply_subtract_fusion.5 = (f32[32,64,1,1,64]{4,1,0,3,2:T(8,128)S(1)}, f32[32,64,1,1,64]{4,1,0,3,2:T(8,128)S(1)}) fusion(f32[32,64,1,1,128]{4,1,0,3,2:T(8,128)S(1)} %dynamic-slice_add_fusion, f32[64]{0:T(128)S(1)} %add_sqrt_fusion.5, f32[32,64]{1,0:T(8,128)S(1)} %add_multiply_fusion.2, f32[64,64]{1,0:T(8,128)} %copy.89, f32[32,64]{1,0:T(8,128)S(1)} %copy.88), kind=kLoop, calls=%fused_computation.56 | loop fusion | flops 1703936 | bytes 2130176 | tf_op jit(solution)/shard_map/sub | solution.py:94
  159.6 6.3 %all-to-all-start = ((f32[32,4,16,128]{3,2,1,0:T(8,128)}), f32[32,4,16,128]{3,2,1,0:T(8,128)S(1)}, u32[]{:S(2)}, u32[]{:S(2)}) async-start(f32[32,4,16,128]{3,2,1,0:T(8,128)} %bitcast.39), calls=%async_computation | async-start | bytes 2097152 | tf_op jit(solution)/shard_map/all_to_all | solution.py:123
  167.3 25.1 %all-to-all-done = f32[32,4,16,128]{3,2,1,0:T(8,128)S(1)} async-done(((f32[32,4,16,128]{3,2,1,0:T(8,128)}), f32[32,4,16,128]{3,2,1,0:T(8,128)S(1)}, u32[]{:S(2)}, u32[]{:S(2)}) %all-to-all-start) | async-done | bytes 1048608 | tf_op jit(solution)/shard_map/all_to_all | solution.py:123
  194.6 18.7 %multiply_subtract_fusion = (f32[16,64,4,2,64]{4,1,3,2,0:T(8,128)S(1)}, f32[16,64,4,2,64]{4,1,3,2,0:T(8,128)S(1)}) fusion(f32[16,64,4,2,128]{4,1,3,2,0:T(8,128)S(1)} %bitcast.116, f32[4,2,64]{2,1,0:T(2,128)S(1)} %add_sqrt_fusion.1, f32[16,64]{1,0:T(8,128)S(1)} %add_multiply_fusion.4, f32[64,2,64]{2,0,1:T(8,128)S(1)} %copy.87, f32[16,4,64]{2,1,0:T(4,128)S(1)} %copy.86), kind=kLoop, calls=%fused_computation.22 | loop fusion | flops 7340032 | bytes 8443904 | tf_op jit(solution)/shard_map/sub | solution.py:94
  214.5 5.2 %copy.110 = f32[16,64,4,2,128]{4,3,2,1,0:T(2,128)} copy(f32[16,64,4,2,128]{4,1,3,2,0:T(8,128)S(1)} %pad_maximum_fusion.2) | data formatting | bytes 8388608 | tf_op jit(solution)/shard_map/concatenate | solution.py:93
  219.7 7.8 %reshape.1693 = f32[16,64,2,512]{3,2,1,0:T(2,128)} reshape(f32[16,64,4,2,128]{4,3,2,1,0:T(2,128)} %copy.110) | data formatting | bytes 8388608 | tf_op jit(solution)/shard_map/reshape.116
  227.5 6.0 %fusion.21 = f32[16,64,2,1,128]{4,1,2,0,3:T(8,128)S(1)} fusion(f32[16,64,2,512]{3,2,1,0:T(2,128)} %reshape.1693, f32[512,128]{1,0:T(8,128)S(1)} %pad_dynamic-update-slice_fusion), kind=kOutput, calls=%fused_computation.43 | convolution fusion | flops 1610612736 | bytes 5505024 | tf_op jit(solution)/shard_map/dot_general | solution.py:108
  233.5 4.6 %multiply_subtract_fusion.4 = (f32[16,64,2,1,64]{4,1,2,0,3:T(8,128)S(1)}, f32[16,64,2,1,64]{4,1,2,0,3:T(8,128)S(1)}) fusion(f32[16,64,2,1,128]{4,1,2,0,3:T(8,128)S(1)} %fusion.21, f32[2,64]{1,0:T(2,128)S(1)} %add_sqrt_fusion.3, f32[16,64]{1,0:T(8,128)S(1)} %add_multiply_fusion.4, f32[64,64]{1,0:T(8,128)S(1)} %copy.85, f32[16,2,64]{2,1,0:T(2,128)S(1)} %copy.84), kind=kLoop, calls=%fused_computation.54 | loop fusion | flops 1703936 | bytes 2126336 | tf_op jit(solution)/shard_map/sub | solution.py:94
  (181 shorter events, 30.7 us)
Async XLA Ops:
  0.0 3.4 %copy-start.1 = (f32[8,16,4,4,128]{4,3,2,1,0:T(4,128)S(1)}, f32[8,16,4,4,128]{4,3,2,1,0:T(4,128)}, u32[]{:S(2)}) copy-start(f32[8,16,4,4,128]{4,3,2,1,0:T(4,128)} %param.1) | copy-start | bytes 3145732
  115.7 2.0 copy-start
  117.8 4.4 %collective-permute-start = (f32[32,128,1,1,128]{4,1,0,3,2:T(8,128)S(1)}, f32[32,128,1,1,128]{4,1,0,3,2:T(8,128)}, u32[]{:S(2)}, u32[]{:S(2)}) collective-permute-start(f32[32,128,1,1,128]{4,1,0,3,2:T(8,128)S(1)} %dynamic-slice_bitcast_fusion), channel_id=1, source_target_pairs={{0,4},{4,0},{8,12},{12,8},{16,20},{20,16},{24,28},{28,24},{1,5},{5... | collective-permute-start | bytes 6291464 | tf_op jit(solution)/shard_map/ppermute | solution.py:22
  119.1 10.4 %copy-start.7 = (f32[16]{0:T(128)}, f32[16]{0:T(128)S(1)}, u32[]{:S(2)}) copy-start(f32[16]{0:T(128)S(1)} %get-tuple-element.65) | copy-start | bytes 196
  124.9 26.5 %collective-permute-start.1 = (f32[32,64,1,1,128]{4,1,0,3,2:T(8,128)S(1)}, f32[32,64,1,1,128]{4,1,0,3,2:T(8,128)}, u32[]{:S(2)}, u32[]{:S(2)}) collective-permute-start(f32[32,64,1,1,128]{4,1,0,3,2:T(8,128)S(1)} %constant_dynamic-slice_fusion), channel_id=1, source_target_pairs={{0,1},{1,0},{2,3},{3,2},{4,5},{5,4},{6,7},{7,6},{8,9},{9,8},{10,11... | collective-permute-start | bytes 3145736 | tf_op jit(solution)/shard_map/ppermute | solution.py:22
  158.1 7.9 %copy-start.6 = (f32[2,8]{1,0:T(2,128)S(1)}, f32[2,8]{1,0:T(2,128)}, u32[]{:S(2)}) copy-start(f32[2,8]{1,0:T(2,128)} %get-tuple-element.30) | copy-start | bytes 196
  158.1 7.9 %copy-start.9 = (f32[64]{0:T(128)S(1)}, f32[64]{0:T(128)}, u32[]{:S(2)}) copy-start(f32[64]{0:T(128)} %get-tuple-element.63) | copy-start | bytes 772
  158.1 7.9 %copy-start.2 = (f32[4,8]{1,0:T(4,128)S(1)}, f32[4,8]{1,0:T(4,128)}, u32[]{:S(2)}) copy-start(f32[4,8]{1,0:T(4,128)} %get-tuple-element.32) | copy-start | bytes 388
  158.1 8.1 %copy-start.5 = (f32[2,8]{1,0:T(2,128)S(1)}, f32[2,8]{1,0:T(2,128)}, u32[]{:S(2)}) copy-start(f32[2,8]{1,0:T(2,128)} %get-tuple-element.28) | copy-start | bytes 196
  158.1 8.3 %copy-start.4 = (f32[2,8]{1,0:T(2,128)S(1)}, f32[2,8]{1,0:T(2,128)}, u32[]{:S(2)}) copy-start(f32[2,8]{1,0:T(2,128)} %get-tuple-element.27) | copy-start | bytes 196
  158.1 8.3 %copy-start.8 = (f32[16]{0:T(128)S(1)}, f32[16]{0:T(128)}, u32[]{:S(2)}) copy-start(f32[16]{0:T(128)} %copy-done.7) | copy-start | bytes 196
  158.1 8.5 %copy-start.3 = (f32[2,8]{1,0:T(2,128)S(1)}, f32[2,8]{1,0:T(2,128)}, u32[]{:S(2)}) copy-start(f32[2,8]{1,0:T(2,128)} %get-tuple-element.29) | copy-start | bytes 196
  158.1 9.1 %copy-start.10 = (f32[16]{0:T(128)S(1)}, f32[16]{0:T(128)}, u32[]{:S(2)}) copy-start(f32[16]{0:T(128)} %get-tuple-element.64) | copy-start | bytes 196
  158.2 9.1 %copy-start.11 = (f32[64]{0:T(128)S(1)}, f32[64]{0:T(128)}, u32[]{:S(2)}) copy-start(f32[64]{0:T(128)} %get-tuple-element.62) | copy-start | bytes 772
  159.6 32.7 %all-to-all-start = ((f32[32,4,16,128]{3,2,1,0:T(8,128)}), f32[32,4,16,128]{3,2,1,0:T(8,128)S(1)}, u32[]{:S(2)}, u32[]{:S(2)}) async-start(f32[32,4,16,128]{3,2,1,0:T(8,128)} %bitcast.39), calls=%async_computation | async-start | bytes 2097152 | tf_op jit(solution)/shard_map/all_to_all | solution.py:123
where the time goes:
time: 245 us; the launch traced here: 241 us
  other arithmetic  103 us (42%)
  local copies, waits for them, and re-layouts  55.6 us (23%)
  waiting for transfers between devices  49.8 us (20%)
  matrix products  21.1 us (9%)
  starting transfers between devices  9.74 us (4%)
    sub x8, other arithmetic, rotate(): cosine * real_part - sine_part * imag_part  89.4 us
    all_to_all x1, waiting for transfers between devices, move_to_targets(): lax.all_to_all(flattened, ('sx', 'sy'), split_axis=0, concat_axis=0, tile...  25.1 us
    ppermute x2, waiting for transfers between devices, swapped(): return lax.ppermute(block, axis, route)  24.8 us
    dot_general x3, matrix products, advance(): jnp.dot(grouped, child_mix, precision=lax.Precision.HIGHEST, preferred_el...  17.3 us
    another operation x2, local copies, waits for them, and re-layouts  14.3 us
    concatenate x2, local copies, waits for them, and re-layouts, rotate(): jnp.concatenate([cosine * real_part - sine_part * imag_part, sine_part *...  10.5 us
    broadcast_in_dim x8, local copies, waits for them, and re-layouts, double_up(): return jnp.repeat(jnp.repeat(values, 2, axis=0), 2, axis=1)  8.24 us
    reshape x1, local copies, waits for them, and re-layouts, advance(): grouped.transpose(0, 1, 2, 4, 3, 5, 6)  6.42 us
  transfers between devices with their start and end apart: 3, of which 3 were waited for; matrix products, arithmetic and copies ran while one was open for 2% of the time, Pallas kernels for 0%

commit v1 on v0

v1 whole, which is shorter than its diff:
```python
import functools

import jax
import jax.numpy as jnp
import ml_dtypes
import numpy as np
from jax import lax
from jax.experimental import pallas as pl
from jax.experimental.pallas import tpu as pltpu
from jax.sharding import PartitionSpec as P

GRID = 4096
BOXES = 64

COS = (0.9999991998413439, -19.738978175861412, 64.92858783993668,
       -85.27084362693975, 58.78694076314819, -21.065429407708887)
SIN = (6.283184911827355, -41.3415883021802, 81.59991361943699,
       -76.61414030097438, 41.34136538557779, -12.468818618521846)

NODES = 0.5 - 0.5 * np.cos(np.pi * (2.0 * np.arange(8) + 1.0) / 16.0)


def mixing():
    def side(c):
        shifted = (c + NODES) / 2.0
        out = np.ones((8, 8))
        for i in range(8):
            for k in range(8):
                if k != i:
                    out[i] *= (shifted - NODES[k]) / (NODES[i] - NODES[k])
        return out

    rows = []
    for cx in range(2):
        for cy in range(2):
            rows.append(np.kron(np.eye(2), np.kron(side(cx), side(cy)).T))
    full = np.concatenate(rows, axis=0)
    high = full.astype(ml_dtypes.bfloat16)
    low = (full - high.astype(np.float64)).astype(ml_dtypes.bfloat16)
    return np.concatenate([high, low], axis=1)


def horner(coefs, z):
    total = coefs[-1] * z + coefs[-2]
    for c in coefs[-3::-1]:
        total = total * z + c
    return total


def sincos(cycles):
    f = cycles - jnp.round(cycles)
    z = f * f
    return f * horner(SIN, z), horner(COS, z)


def sine(cycles):
    f = cycles - jnp.round(cycles)
    return f * horner(SIN, f * f)


def iotas():
    lane = lax.broadcasted_iota(jnp.int32, (8, 128), 1)
    row = lax.broadcasted_iota(jnp.int32, (8, 128), 0)
    return lane, row


def lane_nodes(lane):
    j1 = (lane >> 3) & 7
    j2 = lane & 7
    z1 = jnp.zeros((8, 128), jnp.float32)
    z2 = jnp.zeros((8, 128), jnp.float32)
    for j in range(8):
        z1 = jnp.where(j1 == j, float(NODES[j]), z1)
        z2 = jnp.where(j2 == j, float(NODES[j]), z2)
    return z1, z2


def doubled(value, low_half):
    other = pltpu.roll(value, 64, 1)
    return jnp.where(low_half, value, other), jnp.where(low_half, other, value)


def halves(real, imag):
    both = jnp.concatenate([real, imag], axis=0)
    high = both.astype(jnp.bfloat16)
    return high, (both - high.astype(jnp.float32)).astype(jnp.bfloat16)


def contract(high_ref, low_ref, mix):
    first = jnp.dot(high_ref[...], mix, preferred_element_type=jnp.float32)
    second = jnp.dot(low_ref[...], mix[:, :128], preferred_element_type=jnp.float32)
    return first[:, :128] + first[:, 128:] + second


def turn_back(real, imag, cycles):
    s, c = sincos(cycles)
    return real * c + imag * s, imag * c - real * s


def source_kernel(w_ref, mix_ref, out_ref, amp0, amp1, q_tab, sh, sl, z1_ref):
    a_mid = pl.program_id(0)
    lane, row = iotas()
    low_half = lane < 64
    upper = (lane >> 6) & 1
    pos_x = lax.axis_index("sx")
    pos_y = lax.axis_index("sy")

    @pl.when(a_mid == 0)
    def _():
        z1, z2 = lane_nodes(lane)
        for m in range(4):
            q_tab[m] = (4 * pos_x + m).astype(jnp.float32) + z1
            q_tab[4 + m] = (4 * pos_y + m).astype(jnp.float32) + z2
        for m in range(4):
            for n in range(4):
                amp0[4 * m + n] = 64.0 * jnp.sqrt(q_tab[m] * q_tab[m] + q_tab[4 + n] * q_tab[4 + n])
        sign = jnp.where(low_half, -0.25, 0.25)
        for m in range(2):
            qx = (2 * pos_x + m).astype(jnp.float32) + z1
            q_tab[8 + m] = 0.25 * qx
            for n in range(2):
                qy = (2 * pos_y + n).astype(jnp.float32) + z2
                q_tab[10 + n] = sign * qy
                amp1[2 * m + n] = 128.0 * jnp.sqrt(qx * qx + qy * qy)

    hx = row >> 2
    hy = (row >> 1) & 1
    third = row & 1
    rows0 = hx * 4 + a_mid
    w = w_ref.reshape(8 * 4 * 16, 128)

    def base_column(jb):
        return hy * 8 + jb * 2 + third

    def center(index, total):
        return (index.astype(jnp.float32) + 0.5) * (1.0 / total)

    def level_one(jb, carry):
        columns = base_column(jb) * 2 + upper
        s_y = sine(center(columns, 128))
        shift_y = []
        for n in range(4):
            v = (columns.astype(jnp.float32) + 0.5) * 0.5 * q_tab[4 + n]
            shift_y.append(v - jnp.round(v))
        for s1 in range(2):
            rows = rows0 * 2 + s1
            s_x = sine(center(rows, 128))
            speed = (2.0 + s_x * s_y) * (1.0 / 3.0)
            shift_x = []
            for m in range(4):
                v = (rows.astype(jnp.float32) + 0.5) * 0.5 * q_tab[m]
                shift_x.append(v - jnp.round(v))
            for m in range(4):
                for n in range(4):
                    value = w_ref_load(w, jb, 4 * m + n)
                    other = pltpu.roll(value, 64, 1)
                    real = jnp.where(low_half, value, other)
                    imag = jnp.where(low_half, other, value)
                    cycles = speed * amp0[4 * m + n] + (shift_x[m] + shift_y[n])
                    ure, uim = turn_back(real, imag, cycles)
                    high, low = halves(ure, uim)
                    tile = (s1 * 2 + m // 2) * 2 + n // 2
                    start = pl.multiple_of(jb * 128 + tile * 16, 16)
                    col = (2 * (m % 2) + n % 2) * 128
                    sh[pl.ds(start, 16), col:col + 128] = high
                    sl[pl.ds(start, 16), col:col + 128] = low
        return carry

    def w_ref_load(flat, jb, box):
        parts = [
            flat[pl.ds(((g * 4 + jb) * 2) * 16 + box, 2, stride=16), :] for g in range(4)
        ]
        return jnp.concatenate(parts, axis=0)

    lax.fori_loop(0, 4, level_one, 0)
    z1_ref[...] = contract(sh, sl, mix_ref[...])

    def level_two(jb, carry):
        columns = base_column(jb) * 2
        for s1 in range(2):
            rows = rows0 * 2 + s1
            s_x = sine(center(rows, 128))
            child_x = [sine(center(rows * 2 + t1, 256)) for t1 in range(2)]
            for s2 in range(2):
                s_y = sine(center(columns + s2, 128))
                child_y = sine(center((columns + s2) * 2 + upper, 256))
                for t1 in range(2):
                    change = (child_x[t1] * child_y - s_x * s_y) * (1.0 / 3.0)
                    tile = ((s1 * 4 + jb) * 2 + t1) * 2 + s2
                    start = pl.multiple_of(tile * 16, 16)
                    for c in range(4):
                        source = pl.multiple_of(jb * 128 + (s1 * 4 + c) * 16, 16)
                        real = doubled(z1_ref[pl.ds(source, 8), :], low_half)[s2]
                        imag = doubled(z1_ref[pl.ds(source + 8, 8), :], low_half)[s2]
                        linear = q_tab[10 + c % 2] + (2 * t1 - 1) * q_tab[8 + c // 2]
                        cycles = change * amp1[c] + linear
                        ure, uim = turn_back(real, imag, cycles)
                        high, low = halves(ure, uim)
                        sh[pl.ds(start, 16), c * 128:(c + 1) * 128] = high
                        sl[pl.ds(start, 16), c * 128:(c + 1) * 128] = low
        return carry

    lax.fori_loop(0, 4, level_two, 0)
    out_ref[...] = contract(sh, sl, mix_ref[...])


def source_side(weights, mix):
    pieces = weights.reshape(2, 4, 2, 4, 2, 16, 128)
    return pl.pallas_call(
        source_kernel,
        grid=(4,),
        in_specs=[
            pl.BlockSpec((2, None, 2, 4, 2, 16, 128), lambda a: (0, a, 0, 0, 0, 0, 0)),
            pl.BlockSpec((512, 256), lambda a: (0, 0)),
        ],
        out_specs=pl.BlockSpec((512, 128), lambda a: (a, 0)),
        out_shape=jax.ShapeDtypeStruct((2048, 128), jnp.float32),
        scratch_shapes=[
            pltpu.VMEM((16, 8, 128), jnp.float32),
            pltpu.VMEM((4, 8, 128), jnp.float32),
            pltpu.VMEM((12, 8, 128), jnp.float32),
            pltpu.VMEM((512, 512), jnp.bfloat16),
            pltpu.VMEM((512, 512), jnp.bfloat16),
            pltpu.VMEM((512, 128), jnp.float32),
        ],
        name="source_levels",
        cost_estimate=pl.CostEstimate(flops=2 * 10**9, bytes_accessed=2 * 2**20, transcendentals=0),
    )(pieces, mix)


def target_kernel(nx, ny, piece_x, piece_y, w_ref, mix_ref, out_ref,
                  amp2, lin2, amp3, lin3, amp4, change4, speed4, sh, sl, z3_ref):
    step = pl.program_id(0)
    gx = step // (piece_y // 4)
    gy = step % (piece_y // 4)
    px, py = nx // 2, ny // 2
    fx, fy = nx // 4, ny // 4
    parents = px * py
    lane, row = iotas()
    low_half = lane < 64
    upper = (lane >> 6) & 1
    pos_x = lax.axis_index("sx")
    pos_y = lax.axis_index("sy")
    sign = jnp.where(low_half, -0.25, 0.25)

    @pl.when(step == 0)
    def _():
        z1, z2 = lane_nodes(lane)

        def tables(count_y, scale, amp, lin):
            def one(box, carry):
                qx = (box // count_y).astype(jnp.float32) + z1
                qy = (box % count_y).astype(jnp.float32) + z2
                amp[box] = scale * jnp.sqrt(qx * qx + qy * qy)
                if lin is not None:
                    lin[2 * box] = sign * qy - 0.25 * qx
                    lin[2 * box + 1] = sign * qy + 0.25 * qx
                return carry

            return one

        lax.fori_loop(0, nx * ny, tables(ny, 256.0, amp2, lin2), 0)
        lax.fori_loop(0, px * py, tables(py, 512.0, amp3, lin3), 0)
        lax.fori_loop(0, fx * fy, tables(fy, 1024.0, amp4, None), 0)

    hx = row >> 2
    hy = (row >> 1) & 1
    third = row & 1
    rows2 = hx * 16 + pos_x * piece_x + gx
    cols2 = hy * 32 + pos_y * piece_y + third * (piece_y // 2) + gy * 2

    def center(index, total):
        return (index.astype(jnp.float32) + 0.5) * (1.0 / total)

    change3 = [None] * 4
    s_x2 = sine(center(rows2, 256))
    x3 = [sine(center(2 * rows2 + a1, 512)) for a1 in range(2)]
    x4 = [[sine(center(4 * rows2 + 2 * a1 + b1, 1024)) for b1 in range(2)] for a1 in range(2)]
    for t2 in range(2):
        s_y2 = sine(center(cols2 + t2, 256))
        y3 = sine(center(2 * (cols2 + t2) + upper, 512))
        for a1 in range(2):
            change3[2 * t2 + a1] = (x3[a1] * y3 - s_x2 * s_y2) * (1.0 / 3.0)
            for a2 in range(2):
                y3_own = sine(center(2 * (cols2 + t2) + a2, 512))
                y4 = sine(center(4 * (cols2 + t2) + 2 * a2 + upper, 1024))
                for b1 in range(2):
                    k = ((t2 * 2 + a1) * 2 + a2) * 2 + b1
                    change4[k] = (x4[a1][b1] * y4 - x3[a1] * y3_own) * (1.0 / 3.0)
                    speed4[k] = (2.0 + x4[a1][b1] * y4) * (1.0 / 3.0)

    def level_three(parent, carry):
        m3 = parent // py
        n3 = parent % py
        for c in range(4):
            box = (2 * m3 + c // 2) * ny + 2 * n3 + c % 2
            reals = doubled(w_ref[box, 0:8, :], low_half)
            imags = doubled(w_ref[box, 8:16, :], low_half)
            amp = amp2[box]
            for a1 in range(2):
                lin = lin2[2 * box + a1]
                for t2 in range(2):
                    cycles = change3[2 * t2 + a1] * amp + lin
                    ure, uim = turn_back(reals[t2], imags[t2], cycles)
                    high, low = halves(ure, uim)
                    start = pl.multiple_of(((2 * t2 + a1) * parents + parent) * 16, 16)
                    sh[pl.ds(start, 16), c * 128:(c + 1) * 128] = high
                    sl[pl.ds(start, 16), c * 128:(c + 1) * 128] = low
        return carry

    lax.fori_loop(0, parents, level_three, 0)
    z3_ref[...] = contract(sh, sl, mix_ref[...])

    def level_four(index, carry):
        last = index % (fx * fy)
        ta = index // (fx * fy)
        m4 = last // fy
        n4 = last % fy
        for c in range(4):
            box = (2 * m4 + c // 2) * py + 2 * n4 + c % 2
            source = pl.multiple_of((ta * parents + box) * 16, 16)
            reals = doubled(z3_ref[pl.ds(source, 8), :], low_half)
            imags = doubled(z3_ref[pl.ds(source + 8, 8), :], low_half)
            amp = amp3[box]
            for b1 in range(2):
                lin = lin3[2 * box + b1]
                for a2 in range(2):
                    cycles = change4[ta * 4 + a2 * 2 + b1] * amp + lin
                    ure, uim = turn_back(reals[a2], imags[a2], cycles)
                    high, low = halves(ure, uim)
                    tile = (ta * 4 + a2 * 2 + b1) * (fx * fy) + last
                    start = pl.multiple_of(tile * 16, 16)
                    sh[pl.ds(start, 16), c * 128:(c + 1) * 128] = high
                    sl[pl.ds(start, 16), c * 128:(c + 1) * 128] = low
        return carry

    lax.fori_loop(0, 4 * fx * fy, level_four, 0)
    z3_ref[...] = contract(sh, sl, mix_ref[...])

    boxes = fx * fy
    out = out_ref.reshape(2 * 4 * 4 * 8 * boxes, 128)
    z1, z2 = lane_nodes(lane)

    def finish(index, carry):
        last = index % boxes
        ta = index // boxes
        t2 = ta // 2
        a1 = ta % 2
        p1 = (last // fy).astype(jnp.float32) + z1
        p2 = (last % fy).astype(jnp.float32) + z2
        amp = amp4[last]
        for a2 in range(2):
            col = (4 * (cols2 + t2) + 2 * a2 + upper).astype(jnp.float32) + 0.5
            for b1 in range(2):
                k = ta * 4 + a2 * 2 + b1
                source = pl.multiple_of((k * boxes + last) * 16, 16)
                real = z3_ref[pl.ds(source, 8), :]
                imag = z3_ref[pl.ds(source + 8, 8), :]
                r4 = (4 * rows2 + 2 * a1 + b1).astype(jnp.float32) + 0.5
                cycles = speed4[k] * amp + (r4 * p1 + col * p2)
                s, c = sincos(cycles)
                ore = real * c - imag * s
                oim = real * s + imag * c
                first = jnp.where(low_half, ore, pltpu.roll(oim, 64, 1))
                second = jnp.where(low_half, pltpu.roll(ore, 64, 1), oim)
                for b2, value in enumerate((first, second)):
                    for h in range(2):
                        at = ((h * 4 + 2 * a1 + b1) * 4 * 8 + (4 * t2 + 2 * a2 + b2)) * boxes + last
                        out[pl.ds(at, 4, stride=8 * boxes), :] = value[4 * h:4 * h + 4]
        return carry

    lax.fori_loop(0, 4 * boxes, finish, 0)


def target_side(arrived, mix, nx, ny, piece_x, piece_y):
    fx, fy = nx // 4, ny // 4
    quarter = piece_y // 4
    steps = piece_x * quarter
    rows = 4 * (nx // 2) * (ny // 2) * 16
    return pl.pallas_call(
        functools.partial(target_kernel, nx, ny, piece_x, piece_y),
        grid=(steps,),
        in_specs=[
            pl.BlockSpec((nx * ny, 16, 128), lambda g: (0, g, 0)),
            pl.BlockSpec((512, 256), lambda g: (0, 0)),
        ],
        out_specs=pl.BlockSpec(
            (2, None, 4, 2, 2, None, 8 * fx * fy, 128),
            lambda g: (0, g // quarter, 0, 0, 0, g % quarter, 0, 0),
        ),
        out_shape=jax.ShapeDtypeStruct(
            (2, piece_x, 4, 2, 2, quarter, 8 * fx * fy, 128), jnp.float32
        ),
        scratch_shapes=[
            pltpu.VMEM((nx * ny, 8, 128), jnp.float32),
            pltpu.VMEM((2 * nx * ny, 8, 128), jnp.float32),
            pltpu.VMEM((nx * ny // 4, 8, 128), jnp.float32),
            pltpu.VMEM((nx * ny // 2, 8, 128), jnp.float32),
            pltpu.VMEM((fx * fy, 8, 128), jnp.float32),
            pltpu.VMEM((16, 8, 128), jnp.float32),
            pltpu.VMEM((16, 8, 128), jnp.float32),
            pltpu.VMEM((rows, 512), jnp.bfloat16),
            pltpu.VMEM((rows, 512), jnp.bfloat16),
            pltpu.VMEM((rows, 128), jnp.float32),
        ],
        name="target_levels",
        cost_estimate=pl.CostEstimate(flops=2 * 10**9, bytes_accessed=2 * 2**20, transcendentals=0),
    )(arrived, mix)


def on_device(weights):
    nx = lax.axis_size("sx")
    ny = lax.axis_size("sy")
    piece_x = 2 * weights.shape[0] // nx
    piece_y = 2 * weights.shape[1] // ny
    mix = jnp.asarray(mixing())
    made = source_side(weights, mix)
    if (piece_x, piece_y) != (2, 8):
        made = made.reshape(8, 4, 2, 2, 2, 4, 2, 128)
        lead = [0] + ([2] if piece_x == 1 else []) + [1] + ([6] if piece_y == 4 else [])
        rest = ([2] if piece_x == 2 else []) + ([3] if piece_y == 8 else []) + [4, 5]
        rest += [6] if piece_y == 8 else [3]
        made = made.transpose(lead + rest + [7])
    made = made.reshape(nx * ny, -1, 128)
    arrived = lax.all_to_all(made, ("sx", "sy"), split_axis=0, concat_axis=0, tiled=True)
    out = target_side(arrived, mix, nx, ny, piece_x, piece_y)
    return out.reshape(2, 4 * piece_x, 2, 4 * piece_y, nx // 4, ny // 4, 128)


def solution(mesh):
    return jax.shard_map(
        on_device,
        mesh=mesh,
        in_specs=(P(None, None, "sx", "sy", None),),
        out_specs=P(None, "sx", None, "sy", None, None, None),
        check_vma=False,
    )
```

time: 245 us -> 64 us (0.26); the launches traced: 241 us -> 63.8 us
  other arithmetic: 103 us -> 0 us
  local copies, waits for them, and re-layouts: 55.6 us -> 0 us
  waiting for transfers between devices: 49.8 us -> 0 us
  blocking collectives: 0 us -> 33.9 us
  Pallas kernels: 0 us -> 29.9 us
  matrix products: 21.1 us -> 0 us
  starting transfers between devices: 9.74 us -> 0 us
    sub x10 -> x0, other arithmetic: 89.5 us -> none  [the longest x8 89.4 us: rotate(): cosine * real_part - sine_part * imag_part]
    all_to_all x0 -> x1, blocking collectives: none -> 33.9 us  [on_device(): lax.all_to_all(made, ('sx', 'sy'), split_axis=0, concat_axis=0, tiled=True)]
    pallas_call x0 -> x2, Pallas kernels: none -> 29.9 us  [the longest x1 17.1 us: target_side(): pl.pallas_call(functools.partial(target_kernel, nx, ny, piece_x, piece_y)...]
    all_to_all x1 -> x0, waiting for transfers between devices: 25.1 us -> none  [move_to_targets(): lax.all_to_all(flattened, ('sx', 'sy'), split_axis=0, concat_axis=0, tile...]
    ppermute x2 -> x0, waiting for transfers between devices: 24.8 us -> none  [swapped(): return lax.ppermute(block, axis, route)]
    dot_general x4 -> x0, matrix products: 21.1 us -> none  [the longest x3 17.3 us: advance(): jnp.dot(grouped, child_mix, precision=lax.Precision.HIGHEST, preferred_el...]
    another operation x2 -> x0, local copies, waits for them, and re-layouts: 14.3 us -> none
    concatenate x3 -> x0, local copies, waits for them, and re-layouts: 10.5 us -> none  [the longest x2 10.5 us: rotate(): jnp.concatenate([cosine * real_part - sine_part * imag_part, sine_part *...]
  transfers between devices with their start and end apart: 3 -> 0, of which waited for: 3 -> 0; matrix products, arithmetic and copies ran while one was open for 2% -> 0% of each run, Pallas kernels for 0% -> 0%
where the time goes in v1:
time: 64 us; the launch traced here: 63.8 us
  blocking collectives  33.9 us (53%)
  Pallas kernels  29.9 us (47%)
    all_to_all x1, blocking collectives, on_device(): lax.all_to_all(made, ('sx', 'sy'), split_axis=0, concat_axis=0, tiled=True)  33.9 us
    pallas_call x1, Pallas kernels, target_side(): pl.pallas_call(functools.partial(target_kernel, nx, ny, piece_x, piece_y)...  17.1 us
    pallas_call x1, Pallas kernels, source_side(): pl.pallas_call(source_kernel, grid=(4,), in_specs=[pl.BlockSpec((2, None,...  12.8 us

profile of v1, /device:TPU:0, one launch (start us, length us, event | category | flops | bytes accessed | tf_op | source)
XLA Modules:
  0.0 63.8 jit_solution(2331100694049392149)
XLA Ops:
  0.0 12.8 %source_levels.1 = f32[2048,128]{1,0:T(8,128)} custom-call(f32[2,4,2,4,2,16,128]{6,5,4,3,2,1,0:T(8,128)} %bitcast.6, bf16[512,256]{1,0:T(8,128)(2,1)} %constant.2.clone.mix_ref), custom_call_target="tpu_custom_call" | custom-call | flops 2000000000 | bytes 2097152 | tf_op jit(solution)/shard_map/source_levels/pallas_call | solution.py:209
  12.8 33.9 %all_to_all.5.w_ref = f32[32,64,128]{2,1,0:T(8,128)} all-to-all(f32[32,64,128]{2,1,0:T(8,128)} %bitcast.5), channel_id=1, replica_groups=mesh['sx'=8,'sy'=4] {'sx','sy'}, dimensions={0} | all-to-all | bytes 2097152 | tf_op jit(solution)/shard_map/all_to_all | solution.py:425
  46.6 17.1 %target_levels.1 = f32[2,2,4,2,2,2,16,128]{7,6,5,4,3,2,1,0:T(8,128)} custom-call(f32[32,64,128]{2,1,0:T(8,128)} %all_to_all.5.w_ref, bf16[512,256]{1,0:T(8,128)(2,1)} %constant.2.clone.mix_ref), custom_call_target="tpu_custom_call" | custom-call | flops 2000000000 | bytes 2097152 | tf_op jit(solution)/shard_map/target_levels/pallas_call | solution.py:380

commit v2 on v1

v2 whole, which is shorter than its diff:
```python
import functools

import jax
import jax.numpy as jnp
import ml_dtypes
import numpy as np
from jax import lax
from jax.experimental import pallas as pl
from jax.experimental.pallas import tpu as pltpu
from jax.sharding import PartitionSpec as P

GRID = 4096
BOXES = 64

HALF_SIN = (4.442879586469155, -7.3078180482250685, 3.597788731355218, -0.7912382117199773)
HALF_COS = (1.4142134965649689, -6.978850988233124, 5.739461170564865,
            -1.883562986553834, 0.3106981903146949)

UNROLL = 8

LOW = (True, True, True, True)

NODES = 0.5 - 0.5 * np.cos(np.pi * (2.0 * np.arange(8) + 1.0) / 16.0)


def mixing():
    def side(c):
        shifted = (c + NODES) / 2.0
        out = np.ones((8, 8))
        for i in range(8):
            for k in range(8):
                if k != i:
                    out[i] *= (shifted - NODES[k]) / (NODES[i] - NODES[k])
        return out

    rows = []
    for cx in range(2):
        for cy in range(2):
            rows.append(np.kron(np.eye(2), np.kron(side(cx), side(cy)).T))
    full = np.concatenate(rows, axis=0)
    high = full.astype(ml_dtypes.bfloat16)
    low = (full - high.astype(np.float64)).astype(ml_dtypes.bfloat16)
    return np.concatenate([high, low], axis=1)


def horner(coefs, z):
    total = coefs[-1] * z + coefs[-2]
    for c in coefs[-3::-1]:
        total = total * z + c
    return total


def sincos(cycles):
    f = cycles - jnp.round(cycles)
    z = f * f
    half_sin = f * horner(HALF_SIN, z)
    half_cos = horner(HALF_COS, z)
    return half_sin * half_cos, 1.0 - half_sin * half_sin


def sine(cycles):
    return sincos(cycles)[0]


def iotas():
    lane = lax.broadcasted_iota(jnp.int32, (8, 128), 1)
    row = lax.broadcasted_iota(jnp.int32, (8, 128), 0)
    return lane, row


def lane_nodes(lane):
    j1 = (lane >> 3) & 7
    j2 = lane & 7
    z1 = jnp.zeros((8, 128), jnp.float32)
    z2 = jnp.zeros((8, 128), jnp.float32)
    for j in range(8):
        z1 = jnp.where(j1 == j, float(NODES[j]), z1)
        z2 = jnp.where(j2 == j, float(NODES[j]), z2)
    return z1, z2


def center(index, total):
    return (index.astype(jnp.float32) + 0.5) * (1.0 / total)


def doubled(value, low_half):
    other = pltpu.roll(value, 64, 1)
    return jnp.where(low_half, value, other), jnp.where(low_half, other, value)


def turn_back(real, imag, cycles, buffer, tile, col, low):
    s, c = sincos(cycles)
    both = jnp.concatenate([real * c + imag * s, imag * c - real * s], axis=0)
    high = both.astype(jnp.bfloat16)
    buffer[tile:tile + 16, col:col + 128] = high
    if low:
        rest = both - high.astype(jnp.float32)
        buffer[64 + tile:80 + tile, col:col + 128] = rest.astype(jnp.bfloat16)


def log2(n):
    return n.bit_length() - 1


def staged(count, produce, consume, buffers, mix_ref, low):
    def contracted(buffer):
        rows = buffer[...] if low else buffer[:64, :]
        y = jnp.dot(rows, mix_ref[...], preferred_element_type=jnp.float32)
        total = y[:64, :128] + y[:64, 128:]
        return total + y[64:, :128] if low else total

    produce(jnp.int32(0), buffers[0])

    def body(k, carry):
        for j in range(UNROLL):
            i = k * UNROLL + j
            y = contracted(buffers[j % 2])
            produce(jnp.minimum(i + 1, count - 1), buffers[(j + 1) % 2])
            consume(i, y)
        return carry

    lax.fori_loop(0, count // UNROLL, body, 0)


def source_kernel(w_ref, mix_ref, out_ref, amp0, amp1, q_tab, speed, shift_x, shift_y, change,
                  first, second, z1_ref):
    lane, row = iotas()
    low_half = lane < 64
    upper = (lane >> 6) & 1
    pos_x = lax.axis_index("sx")
    pos_y = lax.axis_index("sy")
    third = 1.0 / 3.0

    z1, z2 = lane_nodes(lane)
    qx0 = [(4 * pos_x + m).astype(jnp.float32) + z1 for m in range(4)]
    qy0 = [(4 * pos_y + n).astype(jnp.float32) + z2 for n in range(4)]
    for m in range(4):
        for n in range(4):
            amp0[4 * m + n] = 64.0 * jnp.sqrt(qx0[m] * qx0[m] + qy0[n] * qy0[n])
    sign = jnp.where(low_half, -0.25, 0.25)
    for m in range(2):
        qx = (2 * pos_x + m).astype(jnp.float32) + z1
        for n in range(2):
            qy = (2 * pos_y + n).astype(jnp.float32) + z2
            amp1[2 * m + n] = 128.0 * jnp.sqrt(qx * qx + qy * qy)
            for t1 in range(2):
                q_tab[2 * (2 * m + n) + t1] = sign * qy + (0.25 * (2 * t1 - 1)) * qx

    hx = row >> 2
    hy = (row >> 1) & 1
    b_low = row & 1
    y_tabs = []
    for jb in range(4):
        column = hy * 8 + jb * 2 + b_low
        both = column * 2 + upper
        for n in range(4):
            v = (both.astype(jnp.float32) + 0.5) * 0.5 * qy0[n]
            shift_y[jb * 4 + n] = v - jnp.round(v)
        own = [sine(center(column * 2 + s2, 128)) for s2 in range(2)]
        child = [sine(center((column * 2 + s2) * 2 + upper, 256)) for s2 in range(2)]
        y_tabs.append((jnp.where(low_half, own[0], own[1]), own, child))

    def tables(i, carry):
        a_mid = i >> 1
        s1 = i & 1
        rows = (hx * 4 + a_mid) * 2 + s1
        s_x = sine(center(rows, 128))
        child_x = [sine(center(rows * 2 + t1, 256)) for t1 in range(2)]
        for m in range(4):
            v = (rows.astype(jnp.float32) + 0.5) * 0.5 * qx0[m]
            shift_x[i * 4 + m] = v - jnp.round(v)
        for jb in range(4):
            both, own, child = y_tabs[jb]
            at = (a_mid * 4 + jb) * 2 + s1
            speed[at] = (2.0 + s_x * both) * third
            for t1 in range(2):
                for s2 in range(2):
                    change[at * 4 + t1 * 2 + s2] = (child_x[t1] * child[s2] - s_x * own[s2]) * third
        return carry

    lax.fori_loop(0, 8, tables, 0)

    def produce_one(i, buffer):
        ajb = i >> 1
        m_half = i & 1
        a_mid = ajb >> 2
        jb = ajb & 3
        for n_half in range(2):
            for cx in range(2):
                m = 2 * m_half + cx
                for cy in range(2):
                    n = 2 * n_half + cy
                    box = 4 * m + n
                    parts = [
                        w_ref[h >> 1, a_mid, h & 1, jb, :, pl.ds(box, 1), :].reshape(2, 128)
                        for h in range(4)
                    ]
                    value = jnp.concatenate(parts, axis=0)
                    other = pltpu.roll(value, 64, 1)
                    real = jnp.where(low_half, value, other)
                    imag = jnp.where(low_half, other, value)
                    amp = amp0[box]
                    for s1 in range(2):
                        shift = shift_x[(a_mid * 2 + s1) * 4 + m] + shift_y[jb * 4 + n]
                        cycles = speed[ajb * 2 + s1] * amp + shift
                        tile = (n_half * 2 + s1) * 16
                        col = (2 * cx + cy) * 128
                        turn_back(real, imag, cycles, buffer, tile, col, LOW[0])

    def consume_one(i, y):
        z1_ref[pl.ds(pl.multiple_of(i * 64, 64), 64), :] = y

    staged(32, produce_one, consume_one, (first, second), mix_ref, LOW[0])

    def produce_two(i, buffer):
        s1 = i & 1
        ajb = i >> 1
        for c in range(4):
            source = pl.multiple_of(((ajb * 4 + c) * 2 + s1) * 16, 16)
            reals = doubled(z1_ref[pl.ds(source, 8), :], low_half)
            imags = doubled(z1_ref[pl.ds(source + 8, 8), :], low_half)
            amp = amp1[c]
            for t1 in range(2):
                lin = q_tab[2 * c + t1]
                for s2 in range(2):
                    cycles = change[i * 4 + t1 * 2 + s2] * amp + lin
                    tile = (t1 * 2 + s2) * 16
                    turn_back(reals[s2], imags[s2], cycles, buffer, tile, c * 128, LOW[1])

    def consume_two(i, y):
        s1 = i & 1
        ajb = i >> 1
        base = pl.multiple_of((((ajb >> 2) * 2 + s1) * 4 + (ajb & 3)) * 64, 64)
        for t1 in range(2):
            for s2 in range(2):
                tile = (t1 * 2 + s2) * 16
                for part in range(2):
                    at = base + (t1 * 32 + part * 16 + s2)
                    out_ref[pl.ds(at, 8, stride=2), :] = y[tile + 8 * part:tile + 8 * part + 8]

    staged(32, produce_two, consume_two, (first, second), mix_ref, LOW[1])


def tab(n):
    return pltpu.VMEM((n, 8, 128), jnp.float32)


def source_side(weights, mix):
    pieces = weights.reshape(2, 4, 2, 4, 2, 16, 128)
    return pl.pallas_call(
        source_kernel,
        in_specs=[pl.BlockSpec(memory_space=pltpu.VMEM)] * 2,
        out_specs=pl.BlockSpec(memory_space=pltpu.VMEM),
        out_shape=jax.ShapeDtypeStruct((2048, 128), jnp.float32),
        scratch_shapes=[
            tab(16), tab(4), tab(8), tab(32), tab(32), tab(16), tab(128),
            pltpu.VMEM((128, 512), jnp.bfloat16),
            pltpu.VMEM((128, 512), jnp.bfloat16),
            pltpu.VMEM((2048, 128), jnp.float32),
        ],
        name="source_levels",
        cost_estimate=pl.CostEstimate(flops=2 * 10**9, bytes_accessed=2 * 2**20, transcendentals=0),
    )(pieces, mix)


def target_kernel(nx, ny, piece_x, piece_y, w_ref, mix_ref, out_ref,
                  amp2, lin2, amp3, lin3, amp4, change3, change4, speed4, first, second, z3_ref):
    px, py = nx // 2, ny // 2
    fx, fy = nx // 4, ny // 4
    parents, boxes = px * py, fx * fy
    wide = piece_y == 8
    groups = piece_x * (2 if wide else 1)
    lane, row = iotas()
    low_half = lane < 64
    upper = (lane >> 6) & 1
    pos_x = lax.axis_index("sx")
    pos_y = lax.axis_index("sy")
    sign = jnp.where(low_half, -0.25, 0.25)
    third = 1.0 / 3.0
    z1, z2 = lane_nodes(lane)

    def box_tables(count_x, count_y, scale, amp, lin):
        qys = [float(n) + z2 for n in range(count_y)]

        def one(m, carry):
            qx = m.astype(jnp.float32) + z1
            for n, qy in enumerate(qys):
                box = m * count_y + n
                amp[box] = scale * jnp.sqrt(qx * qx + qy * qy)
                if lin is not None:
                    lin[2 * box] = sign * qy - 0.25 * qx
                    lin[2 * box + 1] = sign * qy + 0.25 * qx
            return carry

        lax.fori_loop(0, count_x, one, 0)

    box_tables(nx, ny, 256.0, amp2, lin2)
    box_tables(px, py, 512.0, amp3, lin3)
    box_tables(fx, fy, 1024.0, amp4, None)

    if wide:
        hy = row >> 2
        k = row & 3
    else:
        hy = (row >> 1) & 1
        k = row & 1
    cols2 = hy * 32 + pos_y * piece_y + 2 * k

    def rows2(g):
        if wide:
            return jnp.full((8, 128), (g & 1) * 16 + pos_x * piece_x + (g >> 1), jnp.int32)
        return (row >> 2) * 16 + pos_x * piece_x + g

    y_tabs = []
    for t2 in range(2):
        s_y2 = sine(center(cols2 + t2, 256))
        own = [sine(center(2 * (cols2 + t2) + a2, 512)) for a2 in range(2)]
        last = [sine(center(4 * (cols2 + t2) + 2 * a2 + upper, 1024)) for a2 in range(2)]
        y_tabs.append((s_y2, jnp.where(low_half, own[0], own[1]), own, last))

    def target_tables(g, carry):
        rows = rows2(g)
        s_x2 = sine(center(rows, 256))
        for a1 in range(2):
            x3 = sine(center(2 * rows + a1, 512))
            x4 = [sine(center(4 * rows + 2 * a1 + b1, 1024)) for b1 in range(2)]
            for t2 in range(2):
                s_y2, y3, own, last = y_tabs[t2]
                ta = 2 * t2 + a1
                change3[g * 4 + ta] = (x3 * y3 - s_x2 * s_y2) * third
                for a2 in range(2):
                    for b1 in range(2):
                        at = (g * 4 + ta) * 4 + a2 * 2 + b1
                        product = x4[b1] * last[a2]
                        change4[at] = (product - x3 * own[a2]) * third
                        speed4[at] = (2.0 + product) * third
        return carry

    lax.fori_loop(0, groups, target_tables, 0)

    def arrived(box, g, part):
        if wide:
            at = (((g >> 1) * 2 + part) * 2 + (g & 1)) * 8
        else:
            at = (g * 2 + part) * 8
        return w_ref[box, pl.ds(pl.multiple_of(at, 8), 8), :]

    def produce_three(i, buffer):
        g = i >> log2(parents)
        parent = i & (parents - 1)
        m3 = parent >> log2(py)
        n3 = parent & (py - 1)
        for c in range(4):
            box = (2 * m3 + c // 2) * ny + 2 * n3 + c % 2
            reals = doubled(arrived(box, g, 0), low_half)
            imags = doubled(arrived(box, g, 1), low_half)
            amp = amp2[box]
            for a1 in range(2):
                lin = lin2[2 * box + a1]
                for t2 in range(2):
                    ta = 2 * t2 + a1
                    cycles = change3[g * 4 + ta] * amp + lin
                    turn_back(reals[t2], imags[t2], cycles, buffer, ta * 16, c * 128, LOW[2])

    def consume_three(i, y):
        z3_ref[pl.ds(pl.multiple_of(i * 64, 64), 64), :] = y

    staged(groups * parents, produce_three, consume_three, (first, second), mix_ref, LOW[2])

    def decode(i):
        last = i & (boxes - 1)
        gta = i >> log2(boxes)
        return gta >> 2, gta & 3, last

    def produce_four(i, buffer):
        g, ta, last = decode(i)
        m4 = last >> log2(fy)
        n4 = last & (fy - 1)
        for c in range(4):
            box = (2 * m4 + c // 2) * py + 2 * n4 + c % 2
            source = pl.multiple_of(((g * parents + box) * 4 + ta) * 16, 16)
            reals = doubled(z3_ref[pl.ds(source, 8), :], low_half)
            imags = doubled(z3_ref[pl.ds(source + 8, 8), :], low_half)
            amp = amp3[box]
            for b1 in range(2):
                lin = lin3[2 * box + b1]
                for a2 in range(2):
                    tile = a2 * 2 + b1
                    cycles = change4[(g * 4 + ta) * 4 + tile] * amp + lin
                    turn_back(reals[a2], imags[a2], cycles, buffer, tile * 16, c * 128, LOW[3])

    def consume_four(i, y):
        g, ta, last = decode(i)
        t2 = ta >> 1
        a1 = ta & 1
        p1 = (last >> log2(fy)).astype(jnp.float32) + z1
        p2 = (last & (fy - 1)).astype(jnp.float32) + z2
        amp = amp4[last]
        rows = rows2(g) * 4 + 2 * a1
        gx = g >> 1 if wide else g
        for a2 in range(2):
            col = (4 * (cols2 + t2) + 2 * a2 + upper).astype(jnp.float32) + 0.5
            for b1 in range(2):
                tile = a2 * 2 + b1
                real = y[tile * 16:tile * 16 + 8]
                imag = y[tile * 16 + 8:tile * 16 + 16]
                r4 = (rows + b1).astype(jnp.float32) + 0.5
                cycles = speed4[(g * 4 + ta) * 4 + tile] * amp + (r4 * p1 + col * p2)
                s, c = sincos(cycles)
                ore = real * c - imag * s
                oim = real * s + imag * c
                pair = (
                    jnp.where(low_half, ore, pltpu.roll(oim, 64, 1)),
                    jnp.where(low_half, pltpu.roll(ore, 64, 1), oim),
                )
                for b2, value in enumerate(pair):
                    inner = (4 * t2 + 2 * a2 + b2) * boxes + last

                    def at(h):
                        line = (h * piece_x + gx) * 4 + 2 * a1 + b1
                        return line * (piece_y * 8 * boxes) + inner

                    if wide:
                        out_ref[pl.ds(at(g & 1), 8, stride=8 * boxes), :] = value
                    else:
                        for h in range(2):
                            out_ref[pl.ds(at(h), 4, stride=8 * boxes), :] = value[4 * h:4 * h + 4]

    staged(groups * 4 * boxes, produce_four, consume_four, (first, second), mix_ref, LOW[3])


def target_side(arrived, mix, nx, ny, piece_x, piece_y):
    parents, boxes = (nx // 2) * (ny // 2), (nx // 4) * (ny // 4)
    groups = piece_x * (2 if piece_y == 8 else 1)
    return pl.pallas_call(
        functools.partial(target_kernel, nx, ny, piece_x, piece_y),
        in_specs=[pl.BlockSpec(memory_space=pltpu.VMEM)] * 2,
        out_specs=pl.BlockSpec(memory_space=pltpu.VMEM),
        out_shape=jax.ShapeDtypeStruct((2 * 4 * piece_x * 2 * 4 * piece_y * boxes, 128), jnp.float32),
        scratch_shapes=[
            tab(nx * ny), tab(2 * nx * ny), tab(parents), tab(2 * parents), tab(boxes),
            tab(groups * 4), tab(groups * 16), tab(groups * 16),
            pltpu.VMEM((128, 512), jnp.bfloat16),
            pltpu.VMEM((128, 512), jnp.bfloat16),
            pltpu.VMEM((groups * parents * 64, 128), jnp.float32),
        ],
        name="target_levels",
        cost_estimate=pl.CostEstimate(flops=2 * 10**9, bytes_accessed=2 * 2**20, transcendentals=0),
    )(arrived, mix)


def to_targets(made, nx, ny, piece_x, piece_y):
    if (piece_x, piece_y) != (2, 8):
        made = made.reshape(4, 2, 4, 2, 2, 4, 2, 2, 128)
        lead = [0, 1] + ([3] if piece_x == 1 else []) + [2] + ([6] if piece_y == 4 else [])
        rest = ([3] if piece_x == 2 else []) + [4, 5] + ([6] if piece_y == 8 else []) + [7]
        made = made.transpose(lead + rest + [8])
    return made.reshape(nx * ny, -1, 128)


def on_device(weights):
    nx = lax.axis_size("sx")
    ny = lax.axis_size("sy")
    piece_x = 2 * weights.shape[0] // nx
    piece_y = 2 * weights.shape[1] // ny
    mix = jnp.asarray(mixing())
    made = to_targets(source_side(weights, mix), nx, ny, piece_x, piece_y)
    arrived = lax.all_to_all(made, ("sx", "sy"), split_axis=0, concat_axis=0, tiled=True)
    out = target_side(arrived, mix, nx, ny, piece_x, piece_y)
    return out.reshape(2, 4 * piece_x, 2, 4 * piece_y, nx // 4, ny // 4, 128)


def solution(mesh):
    return jax.shard_map(
        on_device,
        mesh=mesh,
        in_specs=(P(None, None, "sx", "sy", None),),
        out_specs=P(None, "sx", None, "sy", None, None, None),
        check_vma=False,
    )
```

time: 64 us -> 55.9 us (0.87)
  Pallas kernels: 29.9 us -> 21.9 us
    pallas_call x1, Pallas kernels: 17.1 us -> 11.1 us  [target_side(): pl.pallas_call(functools.partial(target_kernel, nx, ny, piece_x, piece_y)...]
    pallas_call x1, Pallas kernels: 12.8 us -> 10.7 us  [source_side(): pl.pallas_call(source_kernel, in_specs=[pl.BlockSpec(memory_space=pltpu.V...]
where the time goes in v2:
time: 55.9 us; the launch traced here: 55.7 us
  blocking collectives  33.8 us (60%)
  Pallas kernels  21.9 us (39%)
    all_to_all x1, blocking collectives, on_device(): lax.all_to_all(made, ('sx', 'sy'), split_axis=0, concat_axis=0, tiled=True)  33.8 us
    pallas_call x1, Pallas kernels, target_side(): pl.pallas_call(functools.partial(target_kernel, nx, ny, piece_x, piece_y)...  11.1 us
    pallas_call x1, Pallas kernels, source_side(): pl.pallas_call(source_kernel, in_specs=[pl.BlockSpec(memory_space=pltpu.V...  10.7 us

profile of v2, /device:TPU:0, one launch (start us, length us, event | category | flops | bytes accessed | tf_op | source)
XLA Modules:
  0.0 55.7 jit_solution(12683069695150783751)
XLA Ops:
  0.0 10.7 %source_levels.1 = f32[2048,128]{1,0:T(8,128)} custom-call(f32[2,4,2,4,2,16,128]{6,5,4,3,2,1,0:T(8,128)} %bitcast.6, bf16[512,256]{1,0:T(8,128)(2,1)} %constant.2.clone.mix_ref), custom_call_target="tpu_custom_call" | custom-call | flops 2000000000 | bytes 2097152 | tf_op jit(solution)/shard_map/source_levels/pallas_call | solution.py:250
  10.7 33.8 %all_to_all.5.w_ref = f32[32,64,128]{2,1,0:T(8,128)} all-to-all(f32[32,64,128]{2,1,0:T(8,128)} %bitcast.5), channel_id=1, replica_groups=mesh['sx'=8,'sy'=4] {'sx','sy'}, dimensions={0} | all-to-all | bytes 2097152 | tf_op jit(solution)/shard_map/all_to_all | solution.py:468
  44.6 11.1 %target_levels.1 = f32[2048,128]{1,0:T(8,128)} custom-call(f32[32,64,128]{2,1,0:T(8,128)} %all_to_all.5.w_ref, bf16[512,256]{1,0:T(8,128)(2,1)} %constant.2.clone.mix_ref), custom_call_target="tpu_custom_call" | custom-call | flops 2000000000 | bytes 2097152 | tf_op jit(solution)/shard_map/target_levels/pallas_call | solution.py:435

commit v3 on v2

--- a/solution.py
+++ b/solution.py
@@ -12,9 +12,7 @@
 GRID = 4096
 BOXES = 64
 
-HALF_SIN = (4.442879586469155, -7.3078180482250685, 3.597788731355218, -0.7912382117199773)
-HALF_COS = (1.4142134965649689, -6.978850988233124, 5.739461170564865,
-            -1.883562986553834, 0.3106981903146949)
+HALF_SIN = (4.442867279052734, -7.30741548538208, 3.5945212841033936, -0.7836661338806152)
 
 UNROLL = 8
 
@@ -52,10 +50,10 @@
 
 def sincos(cycles):
     f = cycles - jnp.round(cycles)
-    z = f * f
-    half_sin = f * horner(HALF_SIN, z)
-    half_cos = horner(HALF_COS, z)
-    return half_sin * half_cos, 1.0 - half_sin * half_sin
+    h = f * horner(HALF_SIN, f * f)
+    w = h * h
+    d = 2.0 - w
+    return h * d * lax.rsqrt(d), 1.0 - w
 
 
 def sine(cycles):
@@ -88,42 +86,56 @@
     return jnp.where(low_half, value, other), jnp.where(low_half, other, value)
 
 
-def turn_back(real, imag, cycles, buffer, tile, col, low):
+def turn_back(real, imag, cycles, tiles, tile, child, low):
     s, c = sincos(cycles)
     both = jnp.concatenate([real * c + imag * s, imag * c - real * s], axis=0)
     high = both.astype(jnp.bfloat16)
-    buffer[tile:tile + 16, col:col + 128] = high
+    tiles[tile][child] = high
     if low:
-        rest = both - high.astype(jnp.float32)
-        buffer[64 + tile:80 + tile, col:col + 128] = rest.astype(jnp.bfloat16)
+        tiles[4 + tile][child] = (both - high.astype(jnp.float32)).astype(jnp.bfloat16)
+
+
+def fresh(low):
+    return [[None] * 4 for _ in range(8 if low else 4)]
+
+
+def laid(tiles):
+    return jnp.concatenate([jnp.concatenate(row, axis=1) for row in tiles], axis=0)
 
 
 def log2(n):
     return n.bit_length() - 1
 
 
-def staged(count, produce, consume, buffers, mix_ref, low):
-    def contracted(buffer):
-        rows = buffer[...] if low else buffer[:64, :]
+def staged(count, produce, consume, mix_ref, low, after=None):
+    def contracted(rows):
         y = jnp.dot(rows, mix_ref[...], preferred_element_type=jnp.float32)
         total = y[:64, :128] + y[:64, 128:]
         return total + y[64:, :128] if low else total
 
-    produce(jnp.int32(0), buffers[0])
-
-    def body(k, carry):
+    def body(k, rows):
         for j in range(UNROLL):
             i = k * UNROLL + j
-            y = contracted(buffers[j % 2])
-            produce(jnp.minimum(i + 1, count - 1), buffers[(j + 1) % 2])
+            y = contracted(rows)
+            rows = produce(jnp.minimum(i + 1, count - 1))
             consume(i, y)
-        return carry
-
-    lax.fori_loop(0, count // UNROLL, body, 0)
-
-
-def source_kernel(w_ref, mix_ref, out_ref, amp0, amp1, q_tab, speed, shift_x, shift_y, change,
-                  first, second, z1_ref):
+        if after is not None:
+            after(k)
+        return rows
+
+    lax.fori_loop(0, count // UNROLL, body, produce(jnp.int32(0)))
+
+
+def source_kernel(w_hbm, mix_hbm, out_hbm, amp0, amp1, q_tab, speed, shift_x, shift_y, change,
+                  z1_ref, w_ref, mix_ref, out_ref, in_sem, mix_sem, out_sem):
+    fetches = [
+        pltpu.make_async_copy(w_hbm.at[:, a, :, b], w_ref.at[4 * a + b], in_sem.at[4 * a + b])
+        for a in range(4)
+        for b in range(4)
+    ]
+    fetches.append(pltpu.make_async_copy(mix_hbm, mix_ref, mix_sem))
+    for fetch in fetches:
+        fetch.start()
     lane, row = iotas()
     low_half = lane < 64
     upper = (lane >> 6) & 1
@@ -179,8 +191,12 @@
         return carry
 
     lax.fori_loop(0, 8, tables, 0)
-
-    def produce_one(i, buffer):
+    for fetch in fetches:
+        fetch.wait()
+    w_rows = w_ref.reshape(16 * 128, 128)
+
+    def produce_one(i):
+        tiles = fresh(LOW[0])
         ajb = i >> 1
         m_half = i & 1
         a_mid = ajb >> 2
@@ -191,11 +207,7 @@
                 for cy in range(2):
                     n = 2 * n_half + cy
                     box = 4 * m + n
-                    parts = [
-                        w_ref[h >> 1, a_mid, h & 1, jb, :, pl.ds(box, 1), :].reshape(2, 128)
-                        for h in range(4)
-                    ]
-                    value = jnp.concatenate(parts, axis=0)
+                    value = w_rows[pl.ds(ajb * 128 + box, 8, stride=16), :]
                     other = pltpu.roll(value, 64, 1)
                     real = jnp.where(low_half, value, other)
                     imag = jnp.where(low_half, other, value)
@@ -203,16 +215,16 @@
                     for s1 in range(2):
                         shift = shift_x[(a_mid * 2 + s1) * 4 + m] + shift_y[jb * 4 + n]
                         cycles = speed[ajb * 2 + s1] * amp + shift
-                        tile = (n_half * 2 + s1) * 16
-                        col = (2 * cx + cy) * 128
-                        turn_back(real, imag, cycles, buffer, tile, col, LOW[0])
+                        turn_back(real, imag, cycles, tiles, n_half * 2 + s1, 2 * cx + cy, LOW[0])
+        return laid(tiles)
 
     def consume_one(i, y):
         z1_ref[pl.ds(pl.multiple_of(i * 64, 64), 64), :] = y
 
-    staged(32, produce_one, consume_one, (first, second), mix_ref, LOW[0])
-
-    def produce_two(i, buffer):
+    staged(32, produce_one, consume_one, mix_ref, LOW[0])
+
+    def produce_two(i):
+        tiles = fresh(LOW[1])
         s1 = i & 1
         ajb = i >> 1
         for c in range(4):
@@ -224,8 +236,8 @@
                 lin = q_tab[2 * c + t1]
                 for s2 in range(2):
                     cycles = change[i * 4 + t1 * 2 + s2] * amp + lin
-                    tile = (t1 * 2 + s2) * 16
-                    turn_back(reals[s2], imags[s2], cycles, buffer, tile, c * 128, LOW[1])
+                    turn_back(reals[s2], imags[s2], cycles, tiles, t1 * 2 + s2, c, LOW[1])
+        return laid(tiles)
 
     def consume_two(i, y):
         s1 = i & 1
@@ -238,7 +250,14 @@
                     at = base + (t1 * 32 + part * 16 + s2)
                     out_ref[pl.ds(at, 8, stride=2), :] = y[tile + 8 * part:tile + 8 * part + 8]
 
-    staged(32, produce_two, consume_two, (first, second), mix_ref, LOW[1])
+    def leaving(k):
+        rows = pl.ds(pl.multiple_of(k * 512, 512), 512)
+        return pltpu.make_async_copy(out_ref.at[rows], out_hbm.at[rows], out_sem.at[k])
+
+    staged(32, produce_two, consume_two, mix_ref, LOW[1],
+           lambda k: leaving(k).start())
+    for k in range(4):
+        leaving(k).wait()
 
 
 def tab(n):
@@ -249,22 +268,33 @@
     pieces = weights.reshape(2, 4, 2, 4, 2, 16, 128)
     return pl.pallas_call(
         source_kernel,
-        in_specs=[pl.BlockSpec(memory_space=pltpu.VMEM)] * 2,
-        out_specs=pl.BlockSpec(memory_space=pltpu.VMEM),
+        in_specs=[pl.BlockSpec(memory_space=pl.ANY)] * 2,
+        out_specs=pl.BlockSpec(memory_space=pl.ANY),
         out_shape=jax.ShapeDtypeStruct((2048, 128), jnp.float32),
         scratch_shapes=[
             tab(16), tab(4), tab(8), tab(32), tab(32), tab(16), tab(128),
-            pltpu.VMEM((128, 512), jnp.bfloat16),
-            pltpu.VMEM((128, 512), jnp.bfloat16),
             pltpu.VMEM((2048, 128), jnp.float32),
+            pltpu.VMEM((16, 2, 2, 2, 16, 128), jnp.float32),
+            pltpu.VMEM((512, 256), jnp.bfloat16),
+            pltpu.VMEM((2048, 128), jnp.float32),
+            pltpu.SemaphoreType.DMA((16,)),
+            pltpu.SemaphoreType.DMA,
+            pltpu.SemaphoreType.DMA((4,)),
         ],
         name="source_levels",
         cost_estimate=pl.CostEstimate(flops=2 * 10**9, bytes_accessed=2 * 2**20, transcendentals=0),
     )(pieces, mix)
 
 
-def target_kernel(nx, ny, piece_x, piece_y, w_ref, mix_ref, out_ref,
-                  amp2, lin2, amp3, lin3, amp4, change3, change4, speed4, first, second, z3_ref):
+def target_kernel(nx, ny, piece_x, piece_y, w_hbm, mix_hbm, out_hbm,
+                  amp2, lin2, amp3, lin3, amp4, change3, change4, speed4, z3_ref,
+                  w_ref, mix_ref, out_ref, in_sem, mix_sem, out_sem):
+    fetches = [
+        pltpu.make_async_copy(w_hbm, w_ref, in_sem),
+        pltpu.make_async_copy(mix_hbm, mix_ref, mix_sem),
+    ]
+    for fetch in fetches:
+        fetch.start()
     px, py = nx // 2, ny // 2
     fx, fy = nx // 4, ny // 4
     parents, boxes = px * py, fx * fy
@@ -337,6 +367,8 @@
         return carry
 
     lax.fori_loop(0, groups, target_tables, 0)
+    for fetch in fetches:
+        fetch.wait()
 
     def arrived(box, g, part):
         if wide:
@@ -345,7 +377,8 @@
             at = (g * 2 + part) * 8
         return w_ref[box, pl.ds(pl.multiple_of(at, 8), 8), :]
 
-    def produce_three(i, buffer):
+    def produce_three(i):
+        tiles = fresh(LOW[2])
         g = i >> log2(parents)
         parent = i & (parents - 1)
         m3 = parent >> log2(py)
@@ -360,19 +393,21 @@
                 for t2 in range(2):
                     ta = 2 * t2 + a1
                     cycles = change3[g * 4 + ta] * amp + lin
-                    turn_back(reals[t2], imags[t2], cycles, buffer, ta * 16, c * 128, LOW[2])
+                    turn_back(reals[t2], imags[t2], cycles, tiles, ta, c, LOW[2])
+        return laid(tiles)
 
     def consume_three(i, y):
         z3_ref[pl.ds(pl.multiple_of(i * 64, 64), 64), :] = y
 
-    staged(groups * parents, produce_three, consume_three, (first, second), mix_ref, LOW[2])
+    staged(groups * parents, produce_three, consume_three, mix_ref, LOW[2])
 
     def decode(i):
         last = i & (boxes - 1)
         gta = i >> log2(boxes)
         return gta >> 2, gta & 3, last
 
-    def produce_four(i, buffer):
+    def produce_four(i):
+        tiles = fresh(LOW[3])
         g, ta, last = decode(i)
         m4 = last >> log2(fy)
         n4 = last & (fy - 1)
@@ -387,7 +422,8 @@
                 for a2 in range(2):
                     tile = a2 * 2 + b1
                     cycles = change4[(g * 4 + ta) * 4 + tile] * amp + lin
-                    turn_back(reals[a2], imags[a2], cycles, buffer, tile * 16, c * 128, LOW[3])
+                    turn_back(reals[a2], imags[a2], cycles, tiles, tile, c, LOW[3])
+        return laid(tiles)
 
     def consume_four(i, y):
         g, ta, last = decode(i)
@@ -426,7 +462,21 @@
                         for h in range(2):
                             out_ref[pl.ds(at(h), 4, stride=8 * boxes), :] = value[4 * h:4 * h + 4]
 
-    staged(groups * 4 * boxes, produce_four, consume_four, (first, second), mix_ref, LOW[3])
+    early = wide and 4 * boxes == UNROLL
+    size = 4 * piece_y * 8 * boxes if early else out_hbm.shape[0]
+
+    def leaving(k):
+        if early:
+            k = (k & 1) * piece_x + (k >> 1)
+        rows = pl.ds(pl.multiple_of(k * size, size), size)
+        return pltpu.make_async_copy(out_ref.at[rows], out_hbm.at[rows], out_sem.at[k])
+
+    staged(groups * 4 * boxes, produce_four, consume_four, mix_ref, LOW[3],
+           (lambda k: leaving(k).start()) if early else None)
+    if not early:
+        leaving(0).start()
+    for k in range(groups if early else 1):
+        leaving(k).wait()
 
 
 def target_side(arrived, mix, nx, ny, piece_x, piece_y):
@@ -434,15 +484,19 @@
     groups = piece_x * (2 if piece_y == 8 else 1)
     return pl.pallas_call(
         functools.partial(target_kernel, nx, ny, piece_x, piece_y),
-        in_specs=[pl.BlockSpec(memory_space=pltpu.VMEM)] * 2,
-        out_specs=pl.BlockSpec(memory_space=pltpu.VMEM),
+        in_specs=[pl.BlockSpec(memory_space=pl.ANY)] * 2,
+        out_specs=pl.BlockSpec(memory_space=pl.ANY),
         out_shape=jax.ShapeDtypeStruct((2 * 4 * piece_x * 2 * 4 * piece_y * boxes, 128), jnp.float32),
         scratch_shapes=[
             tab(nx * ny), tab(2 * nx * ny), tab(parents), tab(2 * parents), tab(boxes),
             tab(groups * 4), tab(groups * 16), tab(groups * 16),
-            pltpu.VMEM((128, 512), jnp.bfloat16),
-            pltpu.VMEM((128, 512), jnp.bfloat16),
             pltpu.VMEM((groups * parents * 64, 128), jnp.float32),
+            pltpu.VMEM(arrived.shape, jnp.float32),
+            pltpu.VMEM((512, 256), jnp.bfloat16),
+            pltpu.VMEM((2 * 4 * piece_x * 2 * 4 * piece_y * boxes, 128), jnp.float32),
+            pltpu.SemaphoreType.DMA,
+            pltpu.SemaphoreType.DMA,
+            pltpu.SemaphoreType.DMA((groups,)),
         ],
         name="target_levels",
         cost_estimate=pl.CostEstimate(flops=2 * 10**9, bytes_accessed=2 * 2**20, transcendentals=0),

time: 55.9 us -> 51.5 us (0.921)
  Pallas kernels: 21.9 us -> 17.4 us
    pallas_call x1, Pallas kernels: 10.7 us -> 8.31 us  [source_side(): pl.pallas_call(source_kernel, in_specs=[pl.BlockSpec(memory_space=pl.ANY)...]
    pallas_call x1, Pallas kernels: 11.1 us -> 9.1 us  [target_side(): pl.pallas_call(functools.partial(target_kernel, nx, ny, piece_x, piece_y)...]
where the time goes in v3:
time: 51.5 us; the launch traced here: 51.3 us
  blocking collectives  33.9 us (66%)
  Pallas kernels  17.4 us (34%)
    all_to_all x1, blocking collectives, on_device(): lax.all_to_all(made, ('sx', 'sy'), split_axis=0, concat_axis=0, tiled=True)  33.9 us
    pallas_call x1, Pallas kernels, target_side(): pl.pallas_call(functools.partial(target_kernel, nx, ny, piece_x, piece_y)...  9.1 us
    pallas_call x1, Pallas kernels, source_side(): pl.pallas_call(source_kernel, in_specs=[pl.BlockSpec(memory_space=pl.ANY)...  8.31 us

profile of v3, /device:TPU:0, one launch (start us, length us, event | category | flops | bytes accessed | tf_op | source)
XLA Modules:
  0.0 51.3 jit_solution(14513546296180428484)
XLA Ops:
  0.0 8.3 %source_levels.1 = f32[2048,128]{1,0:T(8,128)} custom-call(f32[2,4,2,4,2,16,128]{6,5,4,3,2,1,0:T(8,128)} %bitcast.6, bf16[512,256]{1,0:T(8,128)(2,1)} %constant.2.clone.mix_hbm), custom_call_target="tpu_custom_call" | custom-call | flops 2000000000 | bytes 2097152 | tf_op jit(solution)/shard_map/source_levels/pallas_call | solution.py:269
  8.3 33.9 %all_to_all.5.w_hbm = f32[32,64,128]{2,1,0:T(8,128)} all-to-all(f32[32,64,128]{2,1,0:T(8,128)} %bitcast.5), channel_id=1, replica_groups=mesh['sx'=8,'sy'=4] {'sx','sy'}, dimensions={0} | all-to-all | bytes 2097152 | tf_op jit(solution)/shard_map/all_to_all | solution.py:522
  42.2 9.1 %target_levels.1 = f32[2048,128]{1,0:T(8,128)} custom-call(f32[32,64,128]{2,1,0:T(8,128)} %all_to_all.5.w_hbm, bf16[512,256]{1,0:T(8,128)(2,1)} %constant.2.clone.mix_hbm), custom_call_target="tpu_custom_call" | custom-call | flops 2000000000 | bytes 2097152 | tf_op jit(solution)/shard_map/target_levels/pallas_call | solution.py:485

commit v4 on v3

--- a/solution.py
+++ b/solution.py
@@ -86,8 +86,7 @@
     return jnp.where(low_half, value, other), jnp.where(low_half, other, value)
 
 
-def turn_back(real, imag, cycles, tiles, tile, child, low):
-    s, c = sincos(cycles)
+def turn_back(real, imag, c, s, tiles, tile, child, low):
     both = jnp.concatenate([real * c + imag * s, imag * c - real * s], axis=0)
     high = both.astype(jnp.bfloat16)
     tiles[tile][child] = high
@@ -107,13 +106,15 @@
     return n.bit_length() - 1
 
 
-def staged(count, produce, consume, mix_ref, low, after=None):
+def staged(count, produce, consume, mix_ref, low, before=None, after=None):
     def contracted(rows):
         y = jnp.dot(rows, mix_ref[...], preferred_element_type=jnp.float32)
         total = y[:64, :128] + y[:64, 128:]
         return total + y[64:, :128] if low else total
 
     def body(k, rows):
+        if before is not None:
+            before(k)
         for j in range(UNROLL):
             i = k * UNROLL + j
             y = contracted(rows)
@@ -215,7 +216,8 @@
                     for s1 in range(2):
                         shift = shift_x[(a_mid * 2 + s1) * 4 + m] + shift_y[jb * 4 + n]
                         cycles = speed[ajb * 2 + s1] * amp + shift
-                        turn_back(real, imag, cycles, tiles, n_half * 2 + s1, 2 * cx + cy, LOW[0])
+                        s, c = sincos(cycles)
+                        turn_back(real, imag, c, s, tiles, n_half * 2 + s1, 2 * cx + cy, LOW[0])
         return laid(tiles)
 
     def consume_one(i, y):
@@ -236,7 +238,8 @@
                 lin = q_tab[2 * c + t1]
                 for s2 in range(2):
                     cycles = change[i * 4 + t1 * 2 + s2] * amp + lin
-                    turn_back(reals[s2], imags[s2], cycles, tiles, t1 * 2 + s2, c, LOW[1])
+                    sin, cos = sincos(cycles)
+                    turn_back(reals[s2], imags[s2], cos, sin, tiles, t1 * 2 + s2, c, LOW[1])
         return laid(tiles)
 
     def consume_two(i, y):
@@ -255,7 +258,7 @@
         return pltpu.make_async_copy(out_ref.at[rows], out_hbm.at[rows], out_sem.at[k])
 
     staged(32, produce_two, consume_two, mix_ref, LOW[1],
-           lambda k: leaving(k).start())
+           after=lambda k: leaving(k).start())
     for k in range(4):
         leaving(k).wait()
 
@@ -286,20 +289,14 @@
     )(pieces, mix)
 
 
-def target_kernel(nx, ny, piece_x, piece_y, w_hbm, mix_hbm, out_hbm,
-                  amp2, lin2, amp3, lin3, amp4, change3, change4, speed4, z3_ref,
-                  w_ref, mix_ref, out_ref, in_sem, mix_sem, out_sem):
-    fetches = [
-        pltpu.make_async_copy(w_hbm, w_ref, in_sem),
-        pltpu.make_async_copy(mix_hbm, mix_ref, mix_sem),
-    ]
-    for fetch in fetches:
-        fetch.start()
-    px, py = nx // 2, ny // 2
-    fx, fy = nx // 4, ny // 4
+def group_bits(nx, ny, piece_x, piece_y):
+    return nx // 2, ny // 2, nx // 4, ny // 4, piece_y == 8, piece_x * (2 if piece_y == 8 else 1)
+
+
+def phase_kernel(nx, ny, piece_x, piece_y, cs3, cs4, cs5,
+                 amp2, lin2, amp3, lin3, amp4, change3, change4, speed4):
+    px, py, fx, fy, wide, groups = group_bits(nx, ny, piece_x, piece_y)
     parents, boxes = px * py, fx * fy
-    wide = piece_y == 8
-    groups = piece_x * (2 if wide else 1)
     lane, row = iotas()
     low_half = lane < 64
     upper = (lane >> 6) & 1
@@ -367,8 +364,100 @@
         return carry
 
     lax.fori_loop(0, groups, target_tables, 0)
-    for fetch in fetches:
-        fetch.wait()
+
+    def put(ref, at, cycles):
+        s, c = sincos(cycles)
+        ref[at] = c
+        ref[at + 1] = s
+
+    def phases_three(i, carry):
+        g = i >> log2(parents)
+        parent = i & (parents - 1)
+        m3 = parent >> log2(py)
+        n3 = parent & (py - 1)
+        for c in range(4):
+            box = (2 * m3 + c // 2) * ny + 2 * n3 + c % 2
+            for ta in range(4):
+                cycles = change3[g * 4 + ta] * amp2[box] + lin2[2 * box + ta % 2]
+                put(cs3, ((i * 4 + c) * 4 + ta) * 2, cycles)
+        return carry
+
+    lax.fori_loop(0, groups * parents, phases_three, 0)
+
+    def phases_four(i, carry):
+        last = i & (boxes - 1)
+        gta = i >> log2(boxes)
+        g = gta >> 2
+        t2 = (gta >> 1) & 1
+        a1 = gta & 1
+        m4 = last >> log2(fy)
+        n4 = last & (fy - 1)
+        p1 = m4.astype(jnp.float32) + z1
+        p2 = n4.astype(jnp.float32) + z2
+        rows = rows2(g) * 4 + 2 * a1
+        for tile in range(4):
+            a2, b1 = tile // 2, tile % 2
+            for c in range(4):
+                box = (2 * m4 + c // 2) * py + 2 * n4 + c % 2
+                cycles = change4[gta * 4 + tile] * amp3[box] + lin3[2 * box + b1]
+                put(cs4, ((i * 4 + c) * 4 + tile) * 2, cycles)
+            col = (4 * (cols2 + t2) + 2 * a2 + upper).astype(jnp.float32) + 0.5
+            r4 = (rows + b1).astype(jnp.float32) + 0.5
+            put(cs5, (i * 4 + tile) * 2, speed4[gta * 4 + tile] * amp4[last] + (r4 * p1 + col * p2))
+        return carry
+
+    lax.fori_loop(0, groups * 4 * boxes, phases_four, 0)
+
+
+def phase_side(nx, ny, piece_x, piece_y):
+    px, py, fx, fy, wide, groups = group_bits(nx, ny, piece_x, piece_y)
+    parents, boxes = px * py, fx * fy
+    items = groups * parents
+    return pl.pallas_call(
+        functools.partial(phase_kernel, nx, ny, piece_x, piece_y),
+        out_specs=[pl.BlockSpec(memory_space=pltpu.VMEM)] * 3,
+        out_shape=[jax.ShapeDtypeStruct((32 * items, 8, 128), jnp.float32), jax.ShapeDtypeStruct((32 * items, 8, 128), jnp.float32),
+                   jax.ShapeDtypeStruct((8 * items, 8, 128), jnp.float32)],
+        scratch_shapes=[
+            tab(nx * ny), tab(2 * nx * ny), tab(parents), tab(2 * parents), tab(boxes),
+            tab(groups * 4), tab(groups * 16), tab(groups * 16),
+        ],
+        name="phases",
+        cost_estimate=pl.CostEstimate(flops=2 * 10**9, bytes_accessed=9 * 2**20, transcendentals=0),
+    )()
+
+
+def target_kernel(nx, ny, piece_x, piece_y, w_ref, mix_ref, cs3_hbm, cs4_hbm, cs5_hbm, out_hbm,
+                  z3_ref, cs3, cs4, cs5, out_ref, in_sem, out_sem):
+    px, py, fx, fy, wide, groups = group_bits(nx, ny, piece_x, piece_y)
+    parents, boxes = px * py, fx * fy
+    low_half = iotas()[0] < 64
+
+    def coming(which, g):
+        source, target = ((cs3_hbm, cs3), (cs4_hbm, cs4), (cs5_hbm, cs5))[which]
+        part = source.shape[0] // groups
+        rows = pl.ds(g * part, part)
+        return pltpu.make_async_copy(source.at[rows], target.at[rows], in_sem.at[which, g])
+
+    for which in range(3):
+        for g in range(groups):
+            coming(which, g).start()
+
+    def await_next(per_group, parts):
+        stepwise = per_group == UNROLL
+        for which in parts:
+            for g in range(1 if stepwise else groups):
+                coming(which, g).wait()
+        if not stepwise:
+            return None
+
+        def before(k):
+            @pl.when(k + 1 < groups)
+            def _():
+                for which in parts:
+                    coming(which, k + 1).wait()
+
+        return before
 
     def arrived(box, g, part):
         if wide:
@@ -387,19 +476,15 @@
             box = (2 * m3 + c // 2) * ny + 2 * n3 + c % 2
             reals = doubled(arrived(box, g, 0), low_half)
             imags = doubled(arrived(box, g, 1), low_half)
-            amp = amp2[box]
-            for a1 in range(2):
-                lin = lin2[2 * box + a1]
-                for t2 in range(2):
-                    ta = 2 * t2 + a1
-                    cycles = change3[g * 4 + ta] * amp + lin
-                    turn_back(reals[t2], imags[t2], cycles, tiles, ta, c, LOW[2])
+            for ta in range(4):
+                at = ((i * 4 + c) * 4 + ta) * 2
+                turn_back(reals[ta // 2], imags[ta // 2], cs3[at], cs3[at + 1], tiles, ta, c, LOW[2])
         return laid(tiles)
 
     def consume_three(i, y):
         z3_ref[pl.ds(pl.multiple_of(i * 64, 64), 64), :] = y
 
-    staged(groups * parents, produce_three, consume_three, mix_ref, LOW[2])
+    staged(groups * parents, produce_three, consume_three, mix_ref, LOW[2], await_next(parents, (0,)))
 
     def decode(i):
         last = i & (boxes - 1)
@@ -416,33 +501,22 @@
             source = pl.multiple_of(((g * parents + box) * 4 + ta) * 16, 16)
             reals = doubled(z3_ref[pl.ds(source, 8), :], low_half)
             imags = doubled(z3_ref[pl.ds(source + 8, 8), :], low_half)
-            amp = amp3[box]
-            for b1 in range(2):
-                lin = lin3[2 * box + b1]
-                for a2 in range(2):
-                    tile = a2 * 2 + b1
-                    cycles = change4[(g * 4 + ta) * 4 + tile] * amp + lin
-                    turn_back(reals[a2], imags[a2], cycles, tiles, tile, c, LOW[3])
+            for tile in range(4):
+                at = ((i * 4 + c) * 4 + tile) * 2
+                turn_back(reals[tile // 2], imags[tile // 2], cs4[at], cs4[at + 1], tiles, tile, c, LOW[3])
         return laid(tiles)
 
     def consume_four(i, y):
         g, ta, last = decode(i)
         t2 = ta >> 1
         a1 = ta & 1
-        p1 = (last >> log2(fy)).astype(jnp.float32) + z1
-        p2 = (last & (fy - 1)).astype(jnp.float32) + z2
-        amp = amp4[last]
-        rows = rows2(g) * 4 + 2 * a1
         gx = g >> 1 if wide else g
         for a2 in range(2):
-            col = (4 * (cols2 + t2) + 2 * a2 + upper).astype(jnp.float32) + 0.5
             for b1 in range(2):
                 tile = a2 * 2 + b1
                 real = y[tile * 16:tile * 16 + 8]
                 imag = y[tile * 16 + 8:tile * 16 + 16]
-                r4 = (rows + b1).astype(jnp.float32) + 0.5
-                cycles = speed4[(g * 4 + ta) * 4 + tile] * amp + (r4 * p1 + col * p2)
-                s, c = sincos(cycles)
+                c, s = cs5[(i * 4 + tile) * 2], cs5[(i * 4 + tile) * 2 + 1]
                 ore = real * c - imag * s
                 oim = real * s + imag * c
                 pair = (
@@ -472,35 +546,31 @@
         return pltpu.make_async_copy(out_ref.at[rows], out_hbm.at[rows], out_sem.at[k])
 
     staged(groups * 4 * boxes, produce_four, consume_four, mix_ref, LOW[3],
-           (lambda k: leaving(k).start()) if early else None)
+           await_next(4 * boxes, (1, 2)), (lambda k: leaving(k).start()) if early else None)
     if not early:
         leaving(0).start()
     for k in range(groups if early else 1):
         leaving(k).wait()
 
 
-def target_side(arrived, mix, nx, ny, piece_x, piece_y):
+def target_side(arrived, mix, phases, nx, ny, piece_x, piece_y):
     parents, boxes = (nx // 2) * (ny // 2), (nx // 4) * (ny // 4)
     groups = piece_x * (2 if piece_y == 8 else 1)
     return pl.pallas_call(
         functools.partial(target_kernel, nx, ny, piece_x, piece_y),
-        in_specs=[pl.BlockSpec(memory_space=pl.ANY)] * 2,
+        in_specs=[pl.BlockSpec(memory_space=pltpu.VMEM)] * 2 + [pl.BlockSpec(memory_space=pl.ANY)] * 3,
         out_specs=pl.BlockSpec(memory_space=pl.ANY),
         out_shape=jax.ShapeDtypeStruct((2 * 4 * piece_x * 2 * 4 * piece_y * boxes, 128), jnp.float32),
         scratch_shapes=[
-            tab(nx * ny), tab(2 * nx * ny), tab(parents), tab(2 * parents), tab(boxes),
-            tab(groups * 4), tab(groups * 16), tab(groups * 16),
             pltpu.VMEM((groups * parents * 64, 128), jnp.float32),
-            pltpu.VMEM(arrived.shape, jnp.float32),
-            pltpu.VMEM((512, 256), jnp.bfloat16),
+            *[pltpu.VMEM(p.shape, jnp.float32) for p in phases],
             pltpu.VMEM((2 * 4 * piece_x * 2 * 4 * piece_y * boxes, 128), jnp.float32),
-            pltpu.SemaphoreType.DMA,
-            pltpu.SemaphoreType.DMA,
+            pltpu.SemaphoreType.DMA((3, groups)),
             pltpu.SemaphoreType.DMA((groups,)),
         ],
         name="target_levels",
         cost_estimate=pl.CostEstimate(flops=2 * 10**9, bytes_accessed=2 * 2**20, transcendentals=0),
-    )(arrived, mix)
+    )(arrived, mix, *phases)
 
 
 def to_targets(made, nx, ny, piece_x, piece_y):
@@ -520,7 +590,8 @@
     mix = jnp.asarray(mixing())
     made = to_targets(source_side(weights, mix), nx, ny, piece_x, piece_y)
     arrived = lax.all_to_all(made, ("sx", "sy"), split_axis=0, concat_axis=0, tiled=True)
-    out = target_side(arrived, mix, nx, ny, piece_x, piece_y)
+    phases = phase_side(nx, ny, piece_x, piece_y)
+    out = target_side(arrived, mix, phases, nx, ny, piece_x, piece_y)
     return out.reshape(2, 4 * piece_x, 2, 4 * piece_y, nx // 4, ny // 4, 128)
 
 

time: 51.5 us -> 51.8 us (level)
  blocking collectives: 33.9 us -> 0 us
  waiting for transfers between devices: 0 us -> 18.8 us
  starting transfers between devices: 0 us -> 7.3 us
  Pallas kernels: 17.4 us -> 24.4 us
  local copies, waits for them, and re-layouts: 0 us -> 1.05 us
    all_to_all x1 -> x0, blocking collectives: 33.9 us -> none  [on_device(): lax.all_to_all(made, ('sx', 'sy'), split_axis=0, concat_axis=0, tiled=True)]
    all_to_all x0 -> x1, waiting for transfers between devices: none -> 18.8 us  [on_device(): lax.all_to_all(made, ('sx', 'sy'), split_axis=0, concat_axis=0, tiled=True)]
    pallas_call x0 -> x1, Pallas kernels: none -> 7.66 us  [phase_side(): pl.pallas_call(functools.partial(phase_kernel, nx, ny, piece_x, piece_y),...]
    all_to_all x0 -> x1, starting transfers between devices: none -> 7.3 us  [on_device(): lax.all_to_all(made, ('sx', 'sy'), split_axis=0, concat_axis=0, tiled=True)]
    unnamed x0 -> x2, local copies, waits for them, and re-layouts: none -> 1.05 us
    pallas_call x1, Pallas kernels: 9.1 us -> 8.39 us  [target_side(): pl.pallas_call(functools.partial(target_kernel, nx, ny, piece_x, piece_y)...]
  transfers between devices with their start and end apart: 0 -> 1, of which waited for: 0 -> 1; matrix products, arithmetic and copies ran while one was open for 0% -> 0% of each run, Pallas kernels for 0% -> 15%
where the time goes in v4:
time: 51.8 us; the launch traced here: 51.5 us
  Pallas kernels  24.4 us (47%)
  waiting for transfers between devices  18.8 us (36%)
  starting transfers between devices  7.3 us (14%)
  local copies, waits for them, and re-layouts  1.05 us (2%)
    all_to_all x1, waiting for transfers between devices, on_device(): lax.all_to_all(made, ('sx', 'sy'), split_axis=0, concat_axis=0, tiled=True)  18.8 us
    pallas_call x1, Pallas kernels, target_side(): pl.pallas_call(functools.partial(target_kernel, nx, ny, piece_x, piece_y)...  8.39 us
    pallas_call x1, Pallas kernels, source_side(): pl.pallas_call(source_kernel, in_specs=[pl.BlockSpec(memory_space=pl.ANY)...  8.31 us
    pallas_call x1, Pallas kernels, phase_side(): pl.pallas_call(functools.partial(phase_kernel, nx, ny, piece_x, piece_y),...  7.66 us
    all_to_all x1, starting transfers between devices, on_device(): lax.all_to_all(made, ('sx', 'sy'), split_axis=0, concat_axis=0, tiled=True)  7.3 us
    unnamed x2, local copies, waits for them, and re-layouts  1.05 us
  transfers between devices with their start and end apart: 1, of which 1 were waited for; matrix products, arithmetic and copies ran while one was open for 0% of the time, Pallas kernels for 15%

profile of v4, /device:TPU:0, one launch (start us, length us, event | category | flops | bytes accessed | tf_op | source)
XLA Modules:
  0.0 51.5 jit_solution(3704033800977755239)
XLA Ops:
  0.0 8.3 %source_levels.1 = f32[2048,128]{1,0:T(8,128)} custom-call(f32[2,4,2,4,2,16,128]{6,5,4,3,2,1,0:T(8,128)} %bitcast.6, bf16[512,256]{1,0:T(8,128)(2,1)} %constant.2.clone.mix_hbm.mix_ref), custom_call_target="tpu_custom_call" | custom-call | flops 2000000000 | bytes 2097152 | tf_op jit(solution)/shard_map/source_levels/pallas_call | solution.py:272
  8.3 7.3 %all-to-all-start = ((f32[32,64,128]{2,1,0:T(8,128)}), f32[32,64,128]{2,1,0:T(8,128)S(1)}, u32[]{:S(2)}, u32[]{:S(2)}) async-start(f32[32,64,128]{2,1,0:T(8,128)} %bitcast.5), calls=%async_computation | async-start | bytes 2097152 | tf_op jit(solution)/shard_map/all_to_all | solution.py:592
  15.6 7.7 %phases.1 = (f32[1024,8,128]{2,1,0:T(8,128)}, f32[1024,8,128]{2,1,0:T(8,128)}, f32[256,8,128]{2,1,0:T(8,128)}) custom-call(), custom_call_target="tpu_custom_call" | custom-call | flops 2000000000 | bytes 9437184 | tf_op jit(solution)/shard_map/phases/pallas_call | solution.py:416
  23.3 18.8 %all-to-all-done.w_ref = f32[32,64,128]{2,1,0:T(8,128)S(1)} async-done(((f32[32,64,128]{2,1,0:T(8,128)}), f32[32,64,128]{2,1,0:T(8,128)S(1)}, u32[]{:S(2)}, u32[]{:S(2)}) %all-to-all-start) | async-done | bytes 1048608 | tf_op jit(solution)/shard_map/all_to_all | solution.py:592
  42.1 0.0 copy-start
  42.1 1.0 %copy-done = f32[32,64,128]{2,1,0:T(8,128)} copy-done((f32[32,64,128]{2,1,0:T(8,128)}, f32[32,64,128]{2,1,0:T(8,128)S(1)}, u32[]{:S(2)}) %copy-start) | copy-done | bytes 1048600
  43.1 8.4 %target_levels.1 = f32[2048,128]{1,0:T(8,128)} custom-call(f32[32,64,128]{2,1,0:T(8,128)} %copy-done, bf16[512,256]{1,0:T(8,128)(2,1)} %constant.2.clone.mix_hbm.mix_ref, f32[1024,8,128]{2,1,0:T(8,128)} %get-tuple-element.8.cs3_hbm, f32[1024,8,128]{2,1,0:T(8,128)} %get-tuple-element.9.cs4_hbm, f32[256,8,128]{2,1,0:T(8,128)} %get-tuple-element.10.cs5_hbm), custom_call_target="tpu_custom_call" | custom-call | flops 2000000000 | bytes 2097152 | tf_op jit(solution)/shard_map/target_levels/pallas_call | solution.py:559
Async XLA Ops:
  8.3 33.7 %all-to-all-start = ((f32[32,64,128]{2,1,0:T(8,128)}), f32[32,64,128]{2,1,0:T(8,128)S(1)}, u32[]{:S(2)}, u32[]{:S(2)}) async-start(f32[32,64,128]{2,1,0:T(8,128)} %bitcast.5), calls=%async_computation | async-start | bytes 2097152 | tf_op jit(solution)/shard_map/all_to_all | solution.py:592
  42.1 1.1 %copy-start = (f32[32,64,128]{2,1,0:T(8,128)}, f32[32,64,128]{2,1,0:T(8,128)S(1)}, u32[]{:S(2)}) copy-start(f32[32,64,128]{2,1,0:T(8,128)S(1)} %all-to-all-done.w_ref) | copy-start | bytes 3145732

commit v5 on v4

--- a/solution.py
+++ b/solution.py
@@ -271,8 +271,8 @@
     pieces = weights.reshape(2, 4, 2, 4, 2, 16, 128)
     return pl.pallas_call(
         source_kernel,
-        in_specs=[pl.BlockSpec(memory_space=pl.ANY)] * 2,
-        out_specs=pl.BlockSpec(memory_space=pl.ANY),
+        in_specs=[pl.BlockSpec(memory_space=pltpu.HBM)] * 2,
+        out_specs=pl.BlockSpec(memory_space=pltpu.HBM),
         out_shape=jax.ShapeDtypeStruct((2048, 128), jnp.float32),
         scratch_shapes=[
             tab(16), tab(4), tab(8), tab(32), tab(32), tab(16), tab(128),
@@ -293,10 +293,17 @@
     return nx // 2, ny // 2, nx // 4, ny // 4, piece_y == 8, piece_x * (2 if piece_y == 8 else 1)
 
 
-def phase_kernel(nx, ny, piece_x, piece_y, cs3, cs4, cs5,
+def ranges(ref, items):
+    return (ref.at[pl.ds(0, 32 * items)], ref.at[pl.ds(32 * items, 32 * items)],
+            ref.at[pl.ds(64 * items, 8 * items)])
+
+
+def phase_kernel(nx, ny, piece_x, piece_y, out_ref,
                  amp2, lin2, amp3, lin3, amp4, change3, change4, speed4):
     px, py, fx, fy, wide, groups = group_bits(nx, ny, piece_x, piece_y)
     parents, boxes = px * py, fx * fy
+    items = groups * parents
+    cs3, cs4, cs5 = ranges(out_ref, items)
     lane, row = iotas()
     low_half = lane < 64
     upper = (lane >> 6) & 1
@@ -415,9 +422,8 @@
     items = groups * parents
     return pl.pallas_call(
         functools.partial(phase_kernel, nx, ny, piece_x, piece_y),
-        out_specs=[pl.BlockSpec(memory_space=pltpu.VMEM)] * 3,
-        out_shape=[jax.ShapeDtypeStruct((32 * items, 8, 128), jnp.float32), jax.ShapeDtypeStruct((32 * items, 8, 128), jnp.float32),
-                   jax.ShapeDtypeStruct((8 * items, 8, 128), jnp.float32)],
+        out_specs=pl.BlockSpec(memory_space=pltpu.VMEM),
+        out_shape=jax.ShapeDtypeStruct((72 * items, 8, 128), jnp.float32),
         scratch_shapes=[
             tab(nx * ny), tab(2 * nx * ny), tab(parents), tab(2 * parents), tab(boxes),
             tab(groups * 4), tab(groups * 16), tab(groups * 16),
@@ -427,14 +433,17 @@
     )()
 
 
-def target_kernel(nx, ny, piece_x, piece_y, w_ref, mix_ref, cs3_hbm, cs4_hbm, cs5_hbm, out_hbm,
-                  z3_ref, cs3, cs4, cs5, out_ref, in_sem, out_sem):
+def target_kernel(nx, ny, piece_x, piece_y, w_ref, mix_ref, cs_hbm, out_hbm,
+                  z3_ref, cs_ref, out_ref, in_sem, out_sem):
     px, py, fx, fy, wide, groups = group_bits(nx, ny, piece_x, piece_y)
     parents, boxes = px * py, fx * fy
     low_half = iotas()[0] < 64
 
+    comes = ranges(cs_hbm, groups * parents)
+    cs3, cs4, cs5 = kept = ranges(cs_ref, groups * parents)
+
     def coming(which, g):
-        source, target = ((cs3_hbm, cs3), (cs4_hbm, cs4), (cs5_hbm, cs5))[which]
+        source, target = comes[which], kept[which]
         part = source.shape[0] // groups
         rows = pl.ds(g * part, part)
         return pltpu.make_async_copy(source.at[rows], target.at[rows], in_sem.at[which, g])
@@ -558,19 +567,20 @@
     groups = piece_x * (2 if piece_y == 8 else 1)
     return pl.pallas_call(
         functools.partial(target_kernel, nx, ny, piece_x, piece_y),
-        in_specs=[pl.BlockSpec(memory_space=pltpu.VMEM)] * 2 + [pl.BlockSpec(memory_space=pl.ANY)] * 3,
-        out_specs=pl.BlockSpec(memory_space=pl.ANY),
+        in_specs=[pl.BlockSpec(memory_space=pltpu.VMEM)] * 2 + [pl.BlockSpec(memory_space=pltpu.HBM)],
+        out_specs=pl.BlockSpec(memory_space=pltpu.HBM),
         out_shape=jax.ShapeDtypeStruct((2 * 4 * piece_x * 2 * 4 * piece_y * boxes, 128), jnp.float32),
         scratch_shapes=[
             pltpu.VMEM((groups * parents * 64, 128), jnp.float32),
-            *[pltpu.VMEM(p.shape, jnp.float32) for p in phases],
+            pltpu.VMEM(phases.shape, jnp.float32),
             pltpu.VMEM((2 * 4 * piece_x * 2 * 4 * piece_y * boxes, 128), jnp.float32),
             pltpu.SemaphoreType.DMA((3, groups)),
             pltpu.SemaphoreType.DMA((groups,)),
         ],
+        compiler_params=pltpu.CompilerParams(vmem_limit_bytes=48 * 2**20),
         name="target_levels",
         cost_estimate=pl.CostEstimate(flops=2 * 10**9, bytes_accessed=2 * 2**20, transcendentals=0),
-    )(arrived, mix, *phases)
+    )(arrived, mix, phases)
 
 
 def to_targets(made, nx, ny, piece_x, piece_y):

time: 51.8 us -> 49.4 us (0.954)
  Pallas kernels: 24.4 us -> 23.2 us
  local copies, waits for them, and re-layouts: 1.05 us -> 0.01 us
    pallas_call x1, Pallas kernels: 8.39 us -> 7.13 us  [target_side(): pl.pallas_call(functools.partial(target_kernel, nx, ny, piece_x, piece_y)...]
    unnamed x2, local copies, waits for them, and re-layouts: 1.05 us -> 0.01 us
  transfers between devices with their start and end apart: 1 -> 1, of which waited for: 1 -> 1; matrix products, arithmetic and copies ran while one was open for 0% -> 0% of each run, Pallas kernels for 15% -> 16%
where the time goes in v5:
time: 49.4 us; the launch traced here: 49.2 us
  Pallas kernels  23.2 us (47%)
  waiting for transfers between devices  18.7 us (38%)
  starting transfers between devices  7.3 us (15%)
    all_to_all x1, waiting for transfers between devices, on_device(): lax.all_to_all(made, ('sx', 'sy'), split_axis=0, concat_axis=0, tiled=True)  18.7 us
    pallas_call x1, Pallas kernels, source_side(): pl.pallas_call(source_kernel, in_specs=[pl.BlockSpec(memory_space=pltpu.H...  8.34 us
    pallas_call x1, Pallas kernels, phase_side(): pl.pallas_call(functools.partial(phase_kernel, nx, ny, piece_x, piece_y),...  7.71 us
    all_to_all x1, starting transfers between devices, on_device(): lax.all_to_all(made, ('sx', 'sy'), split_axis=0, concat_axis=0, tiled=True)  7.3 us
    pallas_call x1, Pallas kernels, target_side(): pl.pallas_call(functools.partial(target_kernel, nx, ny, piece_x, piece_y)...  7.13 us
  transfers between devices with their start and end apart: 1, of which 1 were waited for; matrix products, arithmetic and copies ran while one was open for 0% of the time, Pallas kernels for 16%

profile of v5, /device:TPU:0, one launch (start us, length us, event | category | flops | bytes accessed | tf_op | source)
XLA Modules:
  0.0 49.2 jit_solution(8868251125975129952)
XLA Ops:
  0.0 0.0 copy-start
  0.0 8.3 %source_levels.1 = f32[2048,128]{1,0:T(8,128)} custom-call(f32[2,4,2,4,2,16,128]{6,5,4,3,2,1,0:T(8,128)} %bitcast.6, bf16[512,256]{1,0:T(8,128)(2,1)} %constant.2.clone.mix_hbm.mix_ref), custom_call_target="tpu_custom_call" | custom-call | flops 2000000000 | bytes 2097152 | tf_op jit(solution)/shard_map/source_levels/pallas_call | solution.py:272
  8.3 7.3 %all-to-all-start = ((f32[32,64,128]{2,1,0:T(8,128)}), f32[32,64,128]{2,1,0:T(8,128)S(1)}, u32[]{:S(2)}, u32[]{:S(2)}) async-start(f32[32,64,128]{2,1,0:T(8,128)} %bitcast.5), calls=%async_computation | async-start | bytes 2097152 | tf_op jit(solution)/shard_map/all_to_all | solution.py:602
  15.7 7.7 %phases.1.cs_hbm = f32[2304,8,128]{2,1,0:T(8,128)} custom-call(), custom_call_target="tpu_custom_call" | custom-call | flops 2000000000 | bytes 9437184 | tf_op jit(solution)/shard_map/phases/pallas_call | solution.py:423
  23.4 18.7 %all-to-all-done.w_ref = f32[32,64,128]{2,1,0:T(8,128)S(1)} async-done(((f32[32,64,128]{2,1,0:T(8,128)}), f32[32,64,128]{2,1,0:T(8,128)S(1)}, u32[]{:S(2)}, u32[]{:S(2)}) %all-to-all-start) | async-done | bytes 1048608 | tf_op jit(solution)/shard_map/all_to_all | solution.py:602
  42.1 0.0 copy-done
  42.1 7.1 %target_levels.1 = f32[2048,128]{1,0:T(8,128)} custom-call(f32[32,64,128]{2,1,0:T(8,128)S(1)} %all-to-all-done.w_ref, bf16[512,256]{1,0:T(8,128)(2,1)S(1)} %copy-done, f32[2304,8,128]{2,1,0:T(8,128)} %phases.1.cs_hbm), custom_call_target="tpu_custom_call" | custom-call | flops 2000000000 | bytes 2097152 | tf_op jit(solution)/shard_map/target_levels/pallas_call | solution.py:568
Async XLA Ops:
  0.0 42.1 %copy-start = (bf16[512,256]{1,0:T(8,128)(2,1)S(1)}, bf16[512,256]{1,0:T(8,128)(2,1)}, u32[]{:S(2)}) copy-start(bf16[512,256]{1,0:T(8,128)(2,1)} %constant.2.clone.mix_hbm.mix_ref) | copy-start | bytes 786436
  8.3 33.7 %all-to-all-start = ((f32[32,64,128]{2,1,0:T(8,128)}), f32[32,64,128]{2,1,0:T(8,128)S(1)}, u32[]{:S(2)}, u32[]{:S(2)}) async-start(f32[32,64,128]{2,1,0:T(8,128)} %bitcast.5), calls=%async_computation | async-start | bytes 2097152 | tf_op jit(solution)/shard_map/all_to_all | solution.py:602

commit v6 on v5

--- a/solution.py
+++ b/solution.py
@@ -14,7 +14,9 @@
 
 HALF_SIN = (4.442867279052734, -7.30741548538208, 3.5945212841033936, -0.7836661338806152)
 
-UNROLL = 8
+EARLY = 256
+
+UNROLL = (16, 16, 8, 16)
 
 LOW = (True, True, True, True)
 
@@ -106,7 +108,7 @@
     return n.bit_length() - 1
 
 
-def staged(count, produce, consume, mix_ref, low, before=None, after=None):
+def staged(count, produce, consume, mix_ref, low, unroll, before=None, after=None):
     def contracted(rows):
         y = jnp.dot(rows, mix_ref[...], preferred_element_type=jnp.float32)
         total = y[:64, :128] + y[:64, 128:]
@@ -115,8 +117,8 @@
     def body(k, rows):
         if before is not None:
             before(k)
-        for j in range(UNROLL):
-            i = k * UNROLL + j
+        for j in range(unroll):
+            i = k * unroll + j
             y = contracted(rows)
             rows = produce(jnp.minimum(i + 1, count - 1))
             consume(i, y)
@@ -124,7 +126,7 @@
             after(k)
         return rows
 
-    lax.fori_loop(0, count // UNROLL, body, produce(jnp.int32(0)))
+    lax.fori_loop(0, count // unroll, body, produce(jnp.int32(0)))
 
 
 def source_kernel(w_hbm, mix_hbm, out_hbm, amp0, amp1, q_tab, speed, shift_x, shift_y, change,
@@ -223,7 +225,7 @@
     def consume_one(i, y):
         z1_ref[pl.ds(pl.multiple_of(i * 64, 64), 64), :] = y
 
-    staged(32, produce_one, consume_one, mix_ref, LOW[0])
+    staged(32, produce_one, consume_one, mix_ref, LOW[0], UNROLL[0])
 
     def produce_two(i):
         tiles = fresh(LOW[1])
@@ -254,12 +256,13 @@
                     out_ref[pl.ds(at, 8, stride=2), :] = y[tile + 8 * part:tile + 8 * part + 8]
 
     def leaving(k):
-        rows = pl.ds(pl.multiple_of(k * 512, 512), 512)
+        size = 64 * UNROLL[1]
+        rows = pl.ds(pl.multiple_of(k * size, size), size)
         return pltpu.make_async_copy(out_ref.at[rows], out_hbm.at[rows], out_sem.at[k])
 
-    staged(32, produce_two, consume_two, mix_ref, LOW[1],
+    staged(32, produce_two, consume_two, mix_ref, LOW[1], UNROLL[1],
            after=lambda k: leaving(k).start())
-    for k in range(4):
+    for k in range(32 // UNROLL[1]):
         leaving(k).wait()
 
 
@@ -298,7 +301,7 @@
             ref.at[pl.ds(64 * items, 8 * items)])
 
 
-def phase_kernel(nx, ny, piece_x, piece_y, out_ref,
+def phase_kernel(nx, ny, piece_x, piece_y, out_ref, early_ref,
                  amp2, lin2, amp3, lin3, amp4, change3, change4, speed4):
     px, py, fx, fy, wide, groups = group_bits(nx, ny, piece_x, piece_y)
     parents, boxes = px * py, fx * fy
@@ -390,6 +393,12 @@
         return carry
 
     lax.fori_loop(0, groups * parents, phases_three, 0)
+
+    def early(i, carry):
+        early_ref[pl.ds(i * 8, 8)] = cs3[pl.ds(i * 8, 8)]
+        return carry
+
+    lax.fori_loop(0, early_ref.shape[0] // 8, early, 0)
 
     def phases_four(i, carry):
         last = i & (boxes - 1)
@@ -422,8 +431,9 @@
     items = groups * parents
     return pl.pallas_call(
         functools.partial(phase_kernel, nx, ny, piece_x, piece_y),
-        out_specs=pl.BlockSpec(memory_space=pltpu.VMEM),
-        out_shape=jax.ShapeDtypeStruct((72 * items, 8, 128), jnp.float32),
+        out_specs=[pl.BlockSpec(memory_space=pltpu.VMEM)] * 2,
+        out_shape=[jax.ShapeDtypeStruct((72 * items, 8, 128), jnp.float32),
+                   pltpu.VMEM((EARLY, 8, 128), jnp.float32)],
         scratch_shapes=[
             tab(nx * ny), tab(2 * nx * ny), tab(parents), tab(2 * parents), tab(boxes),
             tab(groups * 4), tab(groups * 16), tab(groups * 16),
@@ -433,7 +443,7 @@
     )()
 
 
-def target_kernel(nx, ny, piece_x, piece_y, w_ref, mix_ref, cs_hbm, out_hbm,
+def target_kernel(nx, ny, piece_x, piece_y, w_ref, mix_ref, early_ref, cs_hbm, out_hbm,
                   z3_ref, cs_ref, out_ref, in_sem, out_sem):
     px, py, fx, fy, wide, groups = group_bits(nx, ny, piece_x, piece_y)
     parents, boxes = px * py, fx * fy
@@ -448,23 +458,42 @@
         rows = pl.ds(g * part, part)
         return pltpu.make_async_copy(source.at[rows], target.at[rows], in_sem.at[which, g])
 
-    for which in range(3):
-        for g in range(groups):
-            coming(which, g).start()
-
-    def await_next(per_group, parts):
-        stepwise = per_group == UNROLL
+    for g in range(1, groups):
+        coming(0, g).start()
+    for g in range(groups):
+        coming(1, g).start()
+        coming(2, g).start()
+    head = 32 * parents
+    if head > EARLY:
+        rest = pl.ds(EARLY, head - EARLY)
+        filling = pltpu.make_async_copy(comes[0].at[rest], cs3.at[rest], in_sem.at[0, 0])
+        filling.start()
+
+    def early(i, carry):
+        cs3[pl.ds(i * 8, 8)] = early_ref[pl.ds(i * 8, 8)]
+        return carry
+
+    lax.fori_loop(0, EARLY // 8, early, 0)
+    if head > EARLY:
+        filling.wait()
+
+    def await_next(per_group, unroll, parts):
+        stepwise = unroll % per_group == 0
         for which in parts:
             for g in range(1 if stepwise else groups):
-                coming(which, g).wait()
+                if (which, g) != (0, 0):
+                    coming(which, g).wait()
         if not stepwise:
             return None
+        each = unroll // per_group
 
         def before(k):
-            @pl.when(k + 1 < groups)
-            def _():
-                for which in parts:
-                    coming(which, k + 1).wait()
+            for n in range(1, each + 1):
+
+                @pl.when(k * each + n < groups)
+                def _():
+                    for which in parts:
+                        coming(which, k * each + n).wait()
 
         return before
 
@@ -493,7 +522,8 @@
     def consume_three(i, y):
         z3_ref[pl.ds(pl.multiple_of(i * 64, 64), 64), :] = y
 
-    staged(groups * parents, produce_three, consume_three, mix_ref, LOW[2], await_next(parents, (0,)))
+    staged(groups * parents, produce_three, consume_three, mix_ref, LOW[2], UNROLL[2],
+           await_next(parents, UNROLL[2], (0,)))
 
     def decode(i):
         last = i & (boxes - 1)
@@ -545,7 +575,8 @@
                         for h in range(2):
                             out_ref[pl.ds(at(h), 4, stride=8 * boxes), :] = value[4 * h:4 * h + 4]
 
-    early = wide and 4 * boxes == UNROLL
+    each = UNROLL[3] // (4 * boxes)
+    early = wide and UNROLL[3] % (4 * boxes) == 0
     size = 4 * piece_y * 8 * boxes if early else out_hbm.shape[0]
 
     def leaving(k):
@@ -554,8 +585,12 @@
         rows = pl.ds(pl.multiple_of(k * size, size), size)
         return pltpu.make_async_copy(out_ref.at[rows], out_hbm.at[rows], out_sem.at[k])
 
-    staged(groups * 4 * boxes, produce_four, consume_four, mix_ref, LOW[3],
-           await_next(4 * boxes, (1, 2)), (lambda k: leaving(k).start()) if early else None)
+    def leave_trip(k):
+        for n in range(each):
+            leaving(k * each + n).start()
+
+    staged(groups * 4 * boxes, produce_four, consume_four, mix_ref, LOW[3], UNROLL[3],
+           await_next(4 * boxes, UNROLL[3], (1, 2)), leave_trip if early else None)
     if not early:
         leaving(0).start()
     for k in range(groups if early else 1):
@@ -567,12 +602,12 @@
     groups = piece_x * (2 if piece_y == 8 else 1)
     return pl.pallas_call(
         functools.partial(target_kernel, nx, ny, piece_x, piece_y),
-        in_specs=[pl.BlockSpec(memory_space=pltpu.VMEM)] * 2 + [pl.BlockSpec(memory_space=pltpu.HBM)],
+        in_specs=[pl.BlockSpec(memory_space=pltpu.VMEM)] * 3 + [pl.BlockSpec(memory_space=pltpu.HBM)],
         out_specs=pl.BlockSpec(memory_space=pltpu.HBM),
         out_shape=jax.ShapeDtypeStruct((2 * 4 * piece_x * 2 * 4 * piece_y * boxes, 128), jnp.float32),
         scratch_shapes=[
             pltpu.VMEM((groups * parents * 64, 128), jnp.float32),
-            pltpu.VMEM(phases.shape, jnp.float32),
+            pltpu.VMEM(phases[0].shape, jnp.float32),
             pltpu.VMEM((2 * 4 * piece_x * 2 * 4 * piece_y * boxes, 128), jnp.float32),
             pltpu.SemaphoreType.DMA((3, groups)),
             pltpu.SemaphoreType.DMA((groups,)),
@@ -580,7 +615,7 @@
         compiler_params=pltpu.CompilerParams(vmem_limit_bytes=48 * 2**20),
         name="target_levels",
         cost_estimate=pl.CostEstimate(flops=2 * 10**9, bytes_accessed=2 * 2**20, transcendentals=0),
-    )(arrived, mix, phases)
+    )(arrived, mix, phases[1], phases[0])
 
 
 def to_targets(made, nx, ny, piece_x, piece_y):

time: 49.4 us -> 48.6 us (0.984)
  Pallas kernels: 23.2 us -> 22.5 us
    pallas_call x1, Pallas kernels: 7.13 us -> 6.53 us  [target_side(): pl.pallas_call(functools.partial(target_kernel, nx, ny, piece_x, piece_y)...]
where the time goes in v6:
time: 48.6 us; the launch traced here: 48.4 us
  Pallas kernels  22.5 us (46%)
  waiting for transfers between devices  18.5 us (38%)
  starting transfers between devices  7.29 us (15%)
    all_to_all x1, waiting for transfers between devices, on_device(): lax.all_to_all(made, ('sx', 'sy'), split_axis=0, concat_axis=0, tiled=True)  18.5 us
    pallas_call x1, Pallas kernels, source_side(): pl.pallas_call(source_kernel, in_specs=[pl.BlockSpec(memory_space=pltpu.H...  8.1 us
    pallas_call x1, Pallas kernels, phase_side(): pl.pallas_call(functools.partial(phase_kernel, nx, ny, piece_x, piece_y),...  7.91 us
    all_to_all x1, starting transfers between devices, on_device(): lax.all_to_all(made, ('sx', 'sy'), split_axis=0, concat_axis=0, tiled=True)  7.29 us
    pallas_call x1, Pallas kernels, target_side(): pl.pallas_call(functools.partial(target_kernel, nx, ny, piece_x, piece_y)...  6.53 us
  transfers between devices with their start and end apart: 1, of which 1 were waited for; matrix products, arithmetic and copies ran while one was open for 0% of the time, Pallas kernels for 16%

profile of v6, /device:TPU:0, one launch (start us, length us, event | category | flops | bytes accessed | tf_op | source)
XLA Modules:
  0.0 48.4 jit_solution(653858430461822375)
XLA Ops:
  0.0 0.0 copy-start
  0.0 8.1 %source_levels.1 = f32[2048,128]{1,0:T(8,128)} custom-call(f32[2,4,2,4,2,16,128]{6,5,4,3,2,1,0:T(8,128)} %bitcast.6, bf16[512,256]{1,0:T(8,128)(2,1)} %constant.2.clone.mix_hbm.mix_ref), custom_call_target="tpu_custom_call" | custom-call | flops 2000000000 | bytes 2097152 | tf_op jit(solution)/shard_map/source_levels/pallas_call | solution.py:275
  8.1 7.3 %all-to-all-start = ((f32[32,64,128]{2,1,0:T(8,128)}), f32[32,64,128]{2,1,0:T(8,128)S(1)}, u32[]{:S(2)}, u32[]{:S(2)}) async-start(f32[32,64,128]{2,1,0:T(8,128)} %bitcast.5), calls=%async_computation | async-start | bytes 2097152 | tf_op jit(solution)/shard_map/all_to_all | solution.py:637
  15.4 7.9 %phases.1 = (f32[2304,8,128]{2,1,0:T(8,128)}, f32[256,8,128]{2,1,0:T(8,128)S(1)}) custom-call(), custom_call_target="tpu_custom_call" | custom-call | flops 2000000000 | bytes 9437184 | tf_op jit(solution)/shard_map/phases/pallas_call | solution.py:432
  23.3 18.5 %all-to-all-done.w_ref = f32[32,64,128]{2,1,0:T(8,128)S(1)} async-done(((f32[32,64,128]{2,1,0:T(8,128)}), f32[32,64,128]{2,1,0:T(8,128)S(1)}, u32[]{:S(2)}, u32[]{:S(2)}) %all-to-all-start) | async-done | bytes 1048608 | tf_op jit(solution)/shard_map/all_to_all | solution.py:637
  41.8 0.0 copy-done
  41.8 6.5 %target_levels.1 = f32[2048,128]{1,0:T(8,128)} custom-call(f32[32,64,128]{2,1,0:T(8,128)S(1)} %all-to-all-done.w_ref, bf16[512,256]{1,0:T(8,128)(2,1)S(1)} %copy-done, f32[256,8,128]{2,1,0:T(8,128)S(1)} %get-tuple-element.7.early_ref, f32[2304,8,128]{2,1,0:T(8,128)} %get-tuple-element.8.cs_hbm), custom_call_target="tpu_custom_call" | custom-call | flops 2000000000 | bytes 2097152 | tf_op jit(solution)/shard_map/target_levels/pallas_call | solution.py:603
Async XLA Ops:
  0.0 41.8 %copy-start = (bf16[512,256]{1,0:T(8,128)(2,1)S(1)}, bf16[512,256]{1,0:T(8,128)(2,1)}, u32[]{:S(2)}) copy-start(bf16[512,256]{1,0:T(8,128)(2,1)} %constant.2.clone.mix_hbm.mix_ref) | copy-start | bytes 786436
  8.1 33.7 %all-to-all-start = ((f32[32,64,128]{2,1,0:T(8,128)}), f32[32,64,128]{2,1,0:T(8,128)S(1)}, u32[]{:S(2)}, u32[]{:S(2)}) async-start(f32[32,64,128]{2,1,0:T(8,128)} %bitcast.5), calls=%async_computation | async-start | bytes 2097152 | tf_op jit(solution)/shard_map/all_to_all | solution.py:637

commit v7 on v6

--- a/solution.py
+++ b/solution.py
@@ -196,7 +196,7 @@
     lax.fori_loop(0, 8, tables, 0)
     for fetch in fetches:
         fetch.wait()
-    w_rows = w_ref.reshape(16 * 128, 128)
+    w_rows = w_ref.reshape(17 * 128, 128)
 
     def produce_one(i):
         tiles = fresh(LOW[0])
@@ -280,9 +280,9 @@
         scratch_shapes=[
             tab(16), tab(4), tab(8), tab(32), tab(32), tab(16), tab(128),
             pltpu.VMEM((2048, 128), jnp.float32),
-            pltpu.VMEM((16, 2, 2, 2, 16, 128), jnp.float32),
+            pltpu.VMEM((17, 2, 2, 2, 16, 128), jnp.float32),
             pltpu.VMEM((512, 256), jnp.bfloat16),
-            pltpu.VMEM((2048, 128), jnp.float32),
+            pltpu.VMEM((2064, 128), jnp.float32),
             pltpu.SemaphoreType.DMA((16,)),
             pltpu.SemaphoreType.DMA,
             pltpu.SemaphoreType.DMA((4,)),
@@ -297,16 +297,15 @@
 
 
 def ranges(ref, items):
-    return (ref.at[pl.ds(0, 32 * items)], ref.at[pl.ds(32 * items, 32 * items)],
-            ref.at[pl.ds(64 * items, 8 * items)])
-
-
-def phase_kernel(nx, ny, piece_x, piece_y, out_ref, early_ref,
+    return ref.at[pl.ds(0, 32 * items)], ref.at[pl.ds(32 * items, 32 * items)]
+
+
+def phase_kernel(nx, ny, piece_x, piece_y, out_ref, early_ref, cs5,
                  amp2, lin2, amp3, lin3, amp4, change3, change4, speed4):
     px, py, fx, fy, wide, groups = group_bits(nx, ny, piece_x, piece_y)
     parents, boxes = px * py, fx * fy
     items = groups * parents
-    cs3, cs4, cs5 = ranges(out_ref, items)
+    cs3, cs4 = ranges(out_ref, items)
     lane, row = iotas()
     low_half = lane < 64
     upper = (lane >> 6) & 1
@@ -431,9 +430,10 @@
     items = groups * parents
     return pl.pallas_call(
         functools.partial(phase_kernel, nx, ny, piece_x, piece_y),
-        out_specs=[pl.BlockSpec(memory_space=pltpu.VMEM)] * 2,
-        out_shape=[jax.ShapeDtypeStruct((72 * items, 8, 128), jnp.float32),
-                   pltpu.VMEM((EARLY, 8, 128), jnp.float32)],
+        out_specs=[pl.BlockSpec(memory_space=pltpu.VMEM)] * 3,
+        out_shape=[jax.ShapeDtypeStruct((64 * items, 8, 128), jnp.float32),
+                   pltpu.VMEM((EARLY, 8, 128), jnp.float32),
+                   pltpu.VMEM((8 * items, 8, 128), jnp.float32)],
         scratch_shapes=[
             tab(nx * ny), tab(2 * nx * ny), tab(parents), tab(2 * parents), tab(boxes),
             tab(groups * 4), tab(groups * 16), tab(groups * 16),
@@ -443,14 +443,14 @@
     )()
 
 
-def target_kernel(nx, ny, piece_x, piece_y, w_ref, mix_ref, early_ref, cs_hbm, out_hbm,
+def target_kernel(nx, ny, piece_x, piece_y, w_ref, mix_ref, early_ref, cs5, cs_hbm, out_hbm,
                   z3_ref, cs_ref, out_ref, in_sem, out_sem):
     px, py, fx, fy, wide, groups = group_bits(nx, ny, piece_x, piece_y)
     parents, boxes = px * py, fx * fy
     low_half = iotas()[0] < 64
 
     comes = ranges(cs_hbm, groups * parents)
-    cs3, cs4, cs5 = kept = ranges(cs_ref, groups * parents)
+    cs3, cs4 = kept = ranges(cs_ref, groups * parents)
 
     def coming(which, g):
         source, target = comes[which], kept[which]
@@ -462,7 +462,6 @@
         coming(0, g).start()
     for g in range(groups):
         coming(1, g).start()
-        coming(2, g).start()
     head = 32 * parents
     if head > EARLY:
         rest = pl.ds(EARLY, head - EARLY)
@@ -590,7 +589,7 @@
             leaving(k * each + n).start()
 
     staged(groups * 4 * boxes, produce_four, consume_four, mix_ref, LOW[3], UNROLL[3],
-           await_next(4 * boxes, UNROLL[3], (1, 2)), leave_trip if early else None)
+           await_next(4 * boxes, UNROLL[3], (1,)), leave_trip if early else None)
     if not early:
         leaving(0).start()
     for k in range(groups if early else 1):
@@ -602,20 +601,20 @@
     groups = piece_x * (2 if piece_y == 8 else 1)
     return pl.pallas_call(
         functools.partial(target_kernel, nx, ny, piece_x, piece_y),
-        in_specs=[pl.BlockSpec(memory_space=pltpu.VMEM)] * 3 + [pl.BlockSpec(memory_space=pltpu.HBM)],
+        in_specs=[pl.BlockSpec(memory_space=pltpu.VMEM)] * 4 + [pl.BlockSpec(memory_space=pltpu.HBM)],
         out_specs=pl.BlockSpec(memory_space=pltpu.HBM),
         out_shape=jax.ShapeDtypeStruct((2 * 4 * piece_x * 2 * 4 * piece_y * boxes, 128), jnp.float32),
         scratch_shapes=[
             pltpu.VMEM((groups * parents * 64, 128), jnp.float32),
             pltpu.VMEM(phases[0].shape, jnp.float32),
-            pltpu.VMEM((2 * 4 * piece_x * 2 * 4 * piece_y * boxes, 128), jnp.float32),
-            pltpu.SemaphoreType.DMA((3, groups)),
+            pltpu.VMEM(((64 * piece_x * piece_y + 64) * boxes, 128), jnp.float32),
+            pltpu.SemaphoreType.DMA((2, groups)),
             pltpu.SemaphoreType.DMA((groups,)),
         ],
         compiler_params=pltpu.CompilerParams(vmem_limit_bytes=48 * 2**20),
         name="target_levels",
         cost_estimate=pl.CostEstimate(flops=2 * 10**9, bytes_accessed=2 * 2**20, transcendentals=0),
-    )(arrived, mix, phases[1], phases[0])
+    )(arrived, mix, phases[1], phases[2], phases[0])
 
 
 def to_targets(made, nx, ny, piece_x, piece_y):

time: 48.6 us -> 48.6 us (level)
  no operation moved by 1% of the time
where the time goes in v7:
time: 48.6 us; the launch traced here: 48.3 us
  Pallas kernels  22.2 us (46%)
  waiting for transfers between devices  18.9 us (39%)
  starting transfers between devices  7.3 us (15%)
    all_to_all x1, waiting for transfers between devices, on_device(): lax.all_to_all(made, ('sx', 'sy'), split_axis=0, concat_axis=0, tiled=True)  18.9 us
    pallas_call x1, Pallas kernels, source_side(): pl.pallas_call(source_kernel, in_specs=[pl.BlockSpec(memory_space=pltpu.H...  8.09 us
    pallas_call x1, Pallas kernels, phase_side(): pl.pallas_call(functools.partial(phase_kernel, nx, ny, piece_x, piece_y),...  7.57 us
    all_to_all x1, starting transfers between devices, on_device(): lax.all_to_all(made, ('sx', 'sy'), split_axis=0, concat_axis=0, tiled=True)  7.3 us
    pallas_call x1, Pallas kernels, target_side(): pl.pallas_call(functools.partial(target_kernel, nx, ny, piece_x, piece_y)...  6.49 us
  transfers between devices with their start and end apart: 1, of which 1 were waited for; matrix products, arithmetic and copies ran while one was open for 0% of the time, Pallas kernels for 16%

profile of v7, /device:TPU:0, one launch (start us, length us, event | category | flops | bytes accessed | tf_op | source)
XLA Modules:
  0.0 48.3 jit_solution(3708771858783193881)
XLA Ops:
  0.0 0.0 copy-start
  0.0 8.1 %source_levels.1 = f32[2048,128]{1,0:T(8,128)} custom-call(f32[2,4,2,4,2,16,128]{6,5,4,3,2,1,0:T(8,128)} %bitcast.6, bf16[512,256]{1,0:T(8,128)(2,1)} %constant.2.clone.mix_hbm.mix_ref), custom_call_target="tpu_custom_call" | custom-call | flops 2000000000 | bytes 2097152 | tf_op jit(solution)/shard_map/source_levels/pallas_call | solution.py:275
  8.1 7.3 %all-to-all-start = ((f32[32,64,128]{2,1,0:T(8,128)}), f32[32,64,128]{2,1,0:T(8,128)S(1)}, u32[]{:S(2)}, u32[]{:S(2)}) async-start(f32[32,64,128]{2,1,0:T(8,128)} %bitcast.5), calls=%async_computation | async-start | bytes 2097152 | tf_op jit(solution)/shard_map/all_to_all | solution.py:636
  15.4 7.6 %phases.1 = (f32[2048,8,128]{2,1,0:T(8,128)}, f32[256,8,128]{2,1,0:T(8,128)S(1)}, f32[256,8,128]{2,1,0:T(8,128)S(1)}) custom-call(), custom_call_target="tpu_custom_call" | custom-call | flops 2000000000 | bytes 9437184 | tf_op jit(solution)/shard_map/phases/pallas_call | solution.py:431
  23.0 18.9 %all-to-all-done.w_ref = f32[32,64,128]{2,1,0:T(8,128)S(1)} async-done(((f32[32,64,128]{2,1,0:T(8,128)}), f32[32,64,128]{2,1,0:T(8,128)S(1)}, u32[]{:S(2)}, u32[]{:S(2)}) %all-to-all-start) | async-done | bytes 1048608 | tf_op jit(solution)/shard_map/all_to_all | solution.py:636
  41.8 0.0 copy-done
  41.9 6.5 %target_levels.1 = f32[2048,128]{1,0:T(8,128)} custom-call(f32[32,64,128]{2,1,0:T(8,128)S(1)} %all-to-all-done.w_ref, bf16[512,256]{1,0:T(8,128)(2,1)S(1)} %copy-done, f32[256,8,128]{2,1,0:T(8,128)S(1)} %get-tuple-element.8.early_ref, f32[256,8,128]{2,1,0:T(8,128)S(1)} %get-tuple-element.9.cs5, f32[2048,8,128]{2,1,0:T(8,128)} %get-tuple-element.10.cs_hbm), custom_call_target="tpu_custom_call" | custom-call | flops 2000000000 | bytes 2097152 | tf_op jit(solution)/shard_map/target_levels/pallas_call | solution.py:602
Async XLA Ops:
  0.0 41.8 %copy-start = (bf16[512,256]{1,0:T(8,128)(2,1)S(1)}, bf16[512,256]{1,0:T(8,128)(2,1)}, u32[]{:S(2)}) copy-start(bf16[512,256]{1,0:T(8,128)(2,1)} %constant.2.clone.mix_hbm.mix_ref) | copy-start | bytes 786436
  8.1 33.7 %all-to-all-start = ((f32[32,64,128]{2,1,0:T(8,128)}), f32[32,64,128]{2,1,0:T(8,128)S(1)}, u32[]{:S(2)}, u32[]{:S(2)}) async-start(f32[32,64,128]{2,1,0:T(8,128)} %bitcast.5), calls=%async_computation | async-start | bytes 2097152 | tf_op jit(solution)/shard_map/all_to_all | solution.py:636

commit v8 on v7

--- a/solution.py
+++ b/solution.py
@@ -16,7 +16,7 @@
 
 EARLY = 256
 
-UNROLL = (16, 16, 8, 16)
+UNROLL = (32, 16, 8, 16)
 
 LOW = (True, True, True, True)
 
@@ -108,7 +108,7 @@
     return n.bit_length() - 1
 
 
-def staged(count, produce, consume, mix_ref, low, unroll, before=None, after=None):
+def staged(count, produce, consume, mix_ref, low, unroll, before=None, after=None, every=8):
     def contracted(rows):
         y = jnp.dot(rows, mix_ref[...], preferred_element_type=jnp.float32)
         total = y[:64, :128] + y[:64, 128:]
@@ -120,13 +120,17 @@
         for j in range(unroll):
             i = k * unroll + j
             y = contracted(rows)
-            rows = produce(jnp.minimum(i + 1, count - 1))
+            if unroll < count or j + 1 < count:
+                rows = produce(jnp.minimum(i + 1, count - 1))
             consume(i, y)
-        if after is not None:
-            after(k)
+            if after is not None and (j + 1) % every == 0:
+                after(k * (unroll // every) + j // every)
         return rows
 
-    lax.fori_loop(0, count // unroll, body, produce(jnp.int32(0)))
+    if unroll == count:
+        body(jnp.int32(0), produce(jnp.int32(0)))
+    else:
+        lax.fori_loop(0, count // unroll, body, produce(jnp.int32(0)))
 
 
 def source_kernel(w_hbm, mix_hbm, out_hbm, amp0, amp1, q_tab, speed, shift_x, shift_y, change,
@@ -256,13 +260,12 @@
                     out_ref[pl.ds(at, 8, stride=2), :] = y[tile + 8 * part:tile + 8 * part + 8]
 
     def leaving(k):
-        size = 64 * UNROLL[1]
-        rows = pl.ds(pl.multiple_of(k * size, size), size)
+        rows = pl.ds(pl.multiple_of(k * 512, 512), 512)
         return pltpu.make_async_copy(out_ref.at[rows], out_hbm.at[rows], out_sem.at[k])
 
     staged(32, produce_two, consume_two, mix_ref, LOW[1], UNROLL[1],
            after=lambda k: leaving(k).start())
-    for k in range(32 // UNROLL[1]):
+    for k in range(4):
         leaving(k).wait()
 
 
@@ -574,8 +577,7 @@
                         for h in range(2):
                             out_ref[pl.ds(at(h), 4, stride=8 * boxes), :] = value[4 * h:4 * h + 4]
 
-    each = UNROLL[3] // (4 * boxes)
-    early = wide and UNROLL[3] % (4 * boxes) == 0
+    early = wide and 4 * boxes == 8
     size = 4 * piece_y * 8 * boxes if early else out_hbm.shape[0]
 
     def leaving(k):
@@ -584,12 +586,8 @@
         rows = pl.ds(pl.multiple_of(k * size, size), size)
         return pltpu.make_async_copy(out_ref.at[rows], out_hbm.at[rows], out_sem.at[k])
 
-    def leave_trip(k):
-        for n in range(each):
-            leaving(k * each + n).start()
-
     staged(groups * 4 * boxes, produce_four, consume_four, mix_ref, LOW[3], UNROLL[3],
-           await_next(4 * boxes, UNROLL[3], (1,)), leave_trip if early else None)
+           await_next(4 * boxes, UNROLL[3], (1,)), (lambda k: leaving(k).start()) if early else None)
     if not early:
         leaving(0).start()
     for k in range(groups if early else 1):

time: 48.6 us -> 48.4 us (level)
  no operation moved by 1% of the time
where the time goes in v8:
time: 48.4 us; the launch traced here: 48.1 us
  Pallas kernels  22 us (45%)
  waiting for transfers between devices  18.9 us (39%)
  starting transfers between devices  7.3 us (15%)
    all_to_all x1, waiting for transfers between devices, on_device(): lax.all_to_all(made, ('sx', 'sy'), split_axis=0, concat_axis=0, tiled=True)  18.9 us
    pallas_call x1, Pallas kernels, source_side(): pl.pallas_call(source_kernel, in_specs=[pl.BlockSpec(memory_space=pltpu.H...  7.98 us
    pallas_call x1, Pallas kernels, phase_side(): pl.pallas_call(functools.partial(phase_kernel, nx, ny, piece_x, piece_y),...  7.57 us
    all_to_all x1, starting transfers between devices, on_device(): lax.all_to_all(made, ('sx', 'sy'), split_axis=0, concat_axis=0, tiled=True)  7.3 us
    pallas_call x1, Pallas kernels, target_side(): pl.pallas_call(functools.partial(target_kernel, nx, ny, piece_x, piece_y)...  6.4 us
  transfers between devices with their start and end apart: 1, of which 1 were waited for; matrix products, arithmetic and copies ran while one was open for 0% of the time, Pallas kernels for 16%

profile of v8, /device:TPU:0, one launch (start us, length us, event | category | flops | bytes accessed | tf_op | source)
XLA Modules:
  0.0 48.1 jit_solution(2389974743043439204)
XLA Ops:
  0.0 0.0 copy-start
  0.0 8.0 %source_levels.1 = f32[2048,128]{1,0:T(8,128)} custom-call(f32[2,4,2,4,2,16,128]{6,5,4,3,2,1,0:T(8,128)} %bitcast.6, bf16[512,256]{1,0:T(8,128)(2,1)} %constant.2.clone.mix_hbm.mix_ref), custom_call_target="tpu_custom_call" | custom-call | flops 2000000000 | bytes 2097152 | tf_op jit(solution)/shard_map/source_levels/pallas_call | solution.py:278
  8.0 7.3 %all-to-all-start = ((f32[32,64,128]{2,1,0:T(8,128)}), f32[32,64,128]{2,1,0:T(8,128)S(1)}, u32[]{:S(2)}, u32[]{:S(2)}) async-start(f32[32,64,128]{2,1,0:T(8,128)} %bitcast.5), calls=%async_computation | async-start | bytes 2097152 | tf_op jit(solution)/shard_map/all_to_all | solution.py:634
  15.3 7.6 %phases.1 = (f32[2048,8,128]{2,1,0:T(8,128)}, f32[256,8,128]{2,1,0:T(8,128)S(1)}, f32[256,8,128]{2,1,0:T(8,128)S(1)}) custom-call(), custom_call_target="tpu_custom_call" | custom-call | flops 2000000000 | bytes 9437184 | tf_op jit(solution)/shard_map/phases/pallas_call | solution.py:434
  22.9 18.9 %all-to-all-done.w_ref = f32[32,64,128]{2,1,0:T(8,128)S(1)} async-done(((f32[32,64,128]{2,1,0:T(8,128)}), f32[32,64,128]{2,1,0:T(8,128)S(1)}, u32[]{:S(2)}, u32[]{:S(2)}) %all-to-all-start) | async-done | bytes 1048608 | tf_op jit(solution)/shard_map/all_to_all | solution.py:634
  41.7 0.0 copy-done
  41.7 6.4 %target_levels.1 = f32[2048,128]{1,0:T(8,128)} custom-call(f32[32,64,128]{2,1,0:T(8,128)S(1)} %all-to-all-done.w_ref, bf16[512,256]{1,0:T(8,128)(2,1)S(1)} %copy-done, f32[256,8,128]{2,1,0:T(8,128)S(1)} %get-tuple-element.8.early_ref, f32[256,8,128]{2,1,0:T(8,128)S(1)} %get-tuple-element.9.cs5, f32[2048,8,128]{2,1,0:T(8,128)} %get-tuple-element.10.cs_hbm), custom_call_target="tpu_custom_call" | custom-call | flops 2000000000 | bytes 2097152 | tf_op jit(solution)/shard_map/target_levels/pallas_call | solution.py:600
Async XLA Ops:
  0.0 41.7 %copy-start = (bf16[512,256]{1,0:T(8,128)(2,1)S(1)}, bf16[512,256]{1,0:T(8,128)(2,1)}, u32[]{:S(2)}) copy-start(bf16[512,256]{1,0:T(8,128)(2,1)} %constant.2.clone.mix_hbm.mix_ref) | copy-start | bytes 786436
  8.0 33.7 %all-to-all-start = ((f32[32,64,128]{2,1,0:T(8,128)}), f32[32,64,128]{2,1,0:T(8,128)S(1)}, u32[]{:S(2)}, u32[]{:S(2)}) async-start(f32[32,64,128]{2,1,0:T(8,128)} %bitcast.5), calls=%async_computation | async-start | bytes 2097152 | tf_op jit(solution)/shard_map/all_to_all | solution.py:634

commit v9 on v8

--- a/solution.py
+++ b/solution.py
@@ -16,7 +16,7 @@
 
 EARLY = 256
 
-UNROLL = (32, 16, 8, 16)
+UNROLL = (32, 32, 8, 16)
 
 LOW = (True, True, True, True)
 

time: 48.4 us -> 48.2 us (level)
  no operation moved by 1% of the time
where the time goes in v9:
time: 48.2 us; the launch traced here: 48 us
  Pallas kernels  21.8 us (45%)
  waiting for transfers between devices  18.9 us (39%)
  starting transfers between devices  7.31 us (15%)
    all_to_all x1, waiting for transfers between devices, on_device(): lax.all_to_all(made, ('sx', 'sy'), split_axis=0, concat_axis=0, tiled=True)  18.9 us
    pallas_call x1, Pallas kernels, source_side(): pl.pallas_call(source_kernel, in_specs=[pl.BlockSpec(memory_space=pltpu.H...  7.82 us
    pallas_call x1, Pallas kernels, phase_side(): pl.pallas_call(functools.partial(phase_kernel, nx, ny, piece_x, piece_y),...  7.57 us
    all_to_all x1, starting transfers between devices, on_device(): lax.all_to_all(made, ('sx', 'sy'), split_axis=0, concat_axis=0, tiled=True)  7.31 us
    pallas_call x1, Pallas kernels, target_side(): pl.pallas_call(functools.partial(target_kernel, nx, ny, piece_x, piece_y)...  6.4 us
  transfers between devices with their start and end apart: 1, of which 1 were waited for; matrix products, arithmetic and copies ran while one was open for 0% of the time, Pallas kernels for 16%

profile of v9, /device:TPU:0, one launch (start us, length us, event | category | flops | bytes accessed | tf_op | source)
XLA Modules:
  0.0 48.0 jit_solution(10663958681499098333)
XLA Ops:
  0.0 0.0 copy-start
  0.0 7.8 %source_levels.1 = f32[2048,128]{1,0:T(8,128)} custom-call(f32[2,4,2,4,2,16,128]{6,5,4,3,2,1,0:T(8,128)} %bitcast.6, bf16[512,256]{1,0:T(8,128)(2,1)} %constant.2.clone.mix_hbm.mix_ref), custom_call_target="tpu_custom_call" | custom-call | flops 2000000000 | bytes 2097152 | tf_op jit(solution)/shard_map/source_levels/pallas_call | solution.py:278
  7.8 7.3 %all-to-all-start = ((f32[32,64,128]{2,1,0:T(8,128)}), f32[32,64,128]{2,1,0:T(8,128)S(1)}, u32[]{:S(2)}, u32[]{:S(2)}) async-start(f32[32,64,128]{2,1,0:T(8,128)} %bitcast.5), calls=%async_computation | async-start | bytes 2097152 | tf_op jit(solution)/shard_map/all_to_all | solution.py:634
  15.1 7.6 %phases.1 = (f32[2048,8,128]{2,1,0:T(8,128)}, f32[256,8,128]{2,1,0:T(8,128)S(1)}, f32[256,8,128]{2,1,0:T(8,128)S(1)}) custom-call(), custom_call_target="tpu_custom_call" | custom-call | flops 2000000000 | bytes 9437184 | tf_op jit(solution)/shard_map/phases/pallas_call | solution.py:434
  22.7 18.9 %all-to-all-done.w_ref = f32[32,64,128]{2,1,0:T(8,128)S(1)} async-done(((f32[32,64,128]{2,1,0:T(8,128)}), f32[32,64,128]{2,1,0:T(8,128)S(1)}, u32[]{:S(2)}, u32[]{:S(2)}) %all-to-all-start) | async-done | bytes 1048608 | tf_op jit(solution)/shard_map/all_to_all | solution.py:634
  41.6 0.0 copy-done
  41.6 6.4 %target_levels.1 = f32[2048,128]{1,0:T(8,128)} custom-call(f32[32,64,128]{2,1,0:T(8,128)S(1)} %all-to-all-done.w_ref, bf16[512,256]{1,0:T(8,128)(2,1)S(1)} %copy-done, f32[256,8,128]{2,1,0:T(8,128)S(1)} %get-tuple-element.8.early_ref, f32[256,8,128]{2,1,0:T(8,128)S(1)} %get-tuple-element.9.cs5, f32[2048,8,128]{2,1,0:T(8,128)} %get-tuple-element.10.cs_hbm), custom_call_target="tpu_custom_call" | custom-call | flops 2000000000 | bytes 2097152 | tf_op jit(solution)/shard_map/target_levels/pallas_call | solution.py:600
Async XLA Ops:
  0.0 41.6 %copy-start = (bf16[512,256]{1,0:T(8,128)(2,1)S(1)}, bf16[512,256]{1,0:T(8,128)(2,1)}, u32[]{:S(2)}) copy-start(bf16[512,256]{1,0:T(8,128)(2,1)} %constant.2.clone.mix_hbm.mix_ref) | copy-start | bytes 786436
  7.8 33.7 %all-to-all-start = ((f32[32,64,128]{2,1,0:T(8,128)}), f32[32,64,128]{2,1,0:T(8,128)S(1)}, u32[]{:S(2)}, u32[]{:S(2)}) async-start(f32[32,64,128]{2,1,0:T(8,128)} %bitcast.5), calls=%async_computation | async-start | bytes 2097152 | tf_op jit(solution)/shard_map/all_to_all | solution.py:634
